TPU v7x, 32 devices: a whole 2x2x4 slice. The times are simulated.
32 devices in a mesh: fsdp: 8 (over z, core), tp: 4 (over y, x).
Axes of the slice: x: 2, y: 2, z: 4, core: 2. Of those that a mesh axis runs over, the one named last changes fastest.
Arguments:
- inputs: float32 [8192, 1024], P(('fsdp', 'tp')), may hold values from -40 to 40
- segment_ids: int32 [8, 1024], P('fsdp'), may hold values from 0 to 15, never falling along the last dimension, each value on 1 to 512 neighbouring positions
- attn_norm: bfloat16 [2, 1024], P(None, 'fsdp'), may hold values from 0.25 to 1.75
- mlp_norm: bfloat16 [2, 1024], P(None, 'fsdp'), may hold values from 0.25 to 1.75
- query_norm: bfloat16 [2, 128], P(None, 'fsdp'), may hold values from 0.25 to 1.75
- key_norm: bfloat16 [2, 128], P(None, 'fsdp'), may hold values from 0.25 to 1.75
- w_query: bfloat16 [2, 1024, 2048], P(None, 'fsdp', 'tp'), may hold values from -0.1875 to 0.1875
- w_key: bfloat16 [2, 1024, 1024], P(None, 'fsdp', 'tp'), may hold values from -0.1875 to 0.1875
- w_value: bfloat16 [2, 1024, 1024], P(None, 'fsdp', 'tp'), may hold values from -0.1875 to 0.1875
- w_out: bfloat16 [2, 2048, 1024], P(None, 'tp', 'fsdp'), may hold values from -0.5 to 0.5
- w_gate: bfloat16 [2, 1024, 3072], P(None, 'fsdp', 'tp'), may hold values from -0.1875 to 0.1875
- w_up: bfloat16 [2, 1024, 3072], P(None, 'fsdp', 'tp'), may hold values from -0.1875 to 0.1875
- w_down: bfloat16 [2, 3072, 1024], P(None, 'tp', 'fsdp'), may hold values from -0.15625 to 0.15625
- cotangent: float32 [8192, 1024], P(('fsdp', 'tp')), may hold values from -6 to 6
Outputs:
- outputs: float32 [8192, 1024], P(('fsdp', 'tp'))
- input_grad: float32 [8192, 1024], P(('fsdp', 'tp'))
- grad_query: float32 [2, 1024, 2048], P(None, 'fsdp', 'tp')
- grad_key: float32 [2, 1024, 1024], P(None, 'fsdp', 'tp')
- grad_value: float32 [2, 1024, 1024], P(None, 'fsdp', 'tp')
- grad_out: float32 [2, 2048, 1024], P(None, 'tp', 'fsdp')
- grad_gate: float32 [2, 1024, 3072], P(None, 'fsdp', 'tp')
- grad_up: float32 [2, 1024, 3072], P(None, 'fsdp', 'tp')
- grad_down: float32 [2, 3072, 1024], P(None, 'tp', 'fsdp')
- grad_attn_norm: float32 [2, 1024], P(None, 'fsdp')
- grad_mlp_norm: float32 [2, 1024], P(None, 'fsdp')
- grad_query_norm: float32 [2, 128], P(None, 'fsdp')
- grad_key_norm: float32 [2, 128], P(None, 'fsdp')
Inputs may be any that keep to these rules, and one draw needn't show every extreme that they name: `segment_ids`: document numbers within each row start at 0 and never fall.
All inputs are finite; a program needn't handle non-finite values.
Results may differ from a plain program's by a relative error of at most 0.03.
Values may be sent and summed in bfloat16 or wider, within the bound.
A program may use at most 256 MiB of HBM per device.

v0:
```python
import math

import jax
import jax.numpy as jnp
from jax import lax
from jax.sharding import PartitionSpec as P

HD = 128


epsilon = 1e-06
theta_base = 1000000.0


def mat_dot(left_arg, right_arg):
    return jnp.dot(left_arg, right_arg, preferred_element_type=jnp.float32)


def dot_left_t(left_arg, right_arg):
    return lax.dot_general(
        left_arg, right_arg, (((0,), (0,)), ((), ())), preferred_element_type=jnp.float32
    )


def dot_right_t(left_arg, right_arg):
    return lax.dot_general(
        left_arg, right_arg, (((1,), (1,)), ((), ())), preferred_element_type=jnp.float32
    )


def positions_of(segment_ids):
    token_index = jnp.arange(segment_ids.shape[1], dtype=jnp.int32)[None, :]
    first_flag = jnp.concatenate(
        [
            jnp.ones((segment_ids.shape[0], 1), dtype=jnp.bool_),
            segment_ids[:, 1:] != segment_ids[:, :-1],
        ],
        axis=1,
    )
    starts = lax.cummax(jnp.where(first_flag, token_index, jnp.zeros_like(token_index)), axis=1)
    return (token_index - starts).reshape(-1)


def rope_tables(positions, head_dim):
    half_dim = head_dim // 2
    frequency = jnp.exp(
        jnp.arange(half_dim, dtype=jnp.float32) * (-2.0 * math.log(theta_base) / head_dim)
    )
    angles = positions.astype(jnp.float32)[:, None] * frequency[None, :]
    return (jnp.cos(angles)[:, None, :], jnp.sin(angles)[:, None, :])


def rope_apply(operand, cosine, sine_part):
    half_dim = operand.shape[-1] // 2
    first_half = operand[..., :half_dim]
    second_half = operand[..., half_dim:]
    return jnp.concatenate(
        [
            first_half * cosine - second_half * sine_part,
            second_half * cosine + first_half * sine_part,
        ],
        axis=-1,
    )


def rope_back(operand, cosine, sine_part):
    half_dim = operand.shape[-1] // 2
    first_half = operand[..., :half_dim]
    second_half = operand[..., half_dim:]
    return jnp.concatenate(
        [
            first_half * cosine + second_half * sine_part,
            second_half * cosine - first_half * sine_part,
        ],
        axis=-1,
    )


def row_norm(operand, gain_vec):
    scale_part = lax.rsqrt(jnp.mean(operand * operand, axis=-1, keepdims=True) + epsilon)
    hat_part = operand * scale_part
    return (hat_part * gain_vec.astype(jnp.float32), hat_part, scale_part)


def norm_back(grad_normed, hat_part, scale_part, gain_vec, sum_axes):
    scaled = grad_normed * gain_vec.astype(jnp.float32)
    grad_in = scale_part * (scaled - hat_part * jnp.mean(scaled * hat_part, axis=-1, keepdims=True))
    grad_gain = jnp.sum(grad_normed * hat_part, axis=sum_axes)
    return (grad_in, grad_gain)


def block_mask(segment_row, row_start, row_stop):
    query_index = jnp.arange(row_start, row_stop, dtype=jnp.int32)
    key_index = jnp.arange(row_stop, dtype=jnp.int32)
    same_doc = segment_row[row_start:row_stop][:, None] == segment_row[:row_stop][None, :]
    return same_doc & (key_index[None, :] <= query_index[:, None])


def block_scores(q_block, k_prefix, segment_row, row_start, row_stop):
    score_scale = q_block.shape[-1] ** (-0.5)
    scores = (
        jnp.einsum("qkgd,tkd->kgqt", q_block, k_prefix, preferred_element_type=jnp.float32)
        * score_scale
    )
    return (scores, block_mask(segment_row, row_start, row_stop), score_scale)


def attend_bundle(bundle):
    q_rot, k_rot, values, segment_row = bundle
    length = q_rot.shape[0]
    block_rows = min(512, length)
    attended_parts = []
    total_parts = []
    for row_start in range(0, length, block_rows):
        row_stop = row_start + block_rows
        scores, allowed, score_scale = block_scores(
            q_rot[row_start:row_stop], k_rot[:row_stop], segment_row, row_start, row_stop
        )
        totals = jnp.sum(jnp.where(allowed, jnp.exp(scores), 0.0), axis=-1)
        log_block = jnp.log(totals)
        attn_probs = jnp.where(allowed, jnp.exp(scores - log_block[..., None]), 0.0)
        attended_parts.append(
            jnp.einsum(
                "kgqt,tkd->qkgd",
                attn_probs.astype(jnp.bfloat16),
                values[:row_stop],
                preferred_element_type=jnp.float32,
            ).astype(jnp.bfloat16)
        )
        total_parts.append(log_block)
    return (jnp.concatenate(attended_parts, axis=0), jnp.concatenate(total_parts, axis=2))


def back_bundle(bundle):
    q_rot, k_rot, values, segment_row, log_total, grad_attended = bundle
    length = q_rot.shape[0]
    block_rows = min(512, length)
    grad_q_parts = []
    grad_k_total = jnp.zeros(k_rot.shape, jnp.float32)
    grad_v_total = jnp.zeros(values.shape, jnp.float32)
    for row_start in range(0, length, block_rows):
        row_stop = row_start + block_rows
        pad_rows = ((0, length - row_stop), (0, 0), (0, 0))
        scores, allowed, score_scale = block_scores(
            q_rot[row_start:row_stop], k_rot[:row_stop], segment_row, row_start, row_stop
        )
        attn_probs = jnp.where(
            allowed, jnp.exp(scores - log_total[:, :, row_start:row_stop, None]), 0.0
        )
        grad_block = grad_attended[row_start:row_stop]
        grad_v_piece = jnp.einsum(
            "kgqt,qkgd->tkd",
            attn_probs.astype(jnp.bfloat16),
            grad_block,
            preferred_element_type=jnp.float32,
        )
        grad_v_total = grad_v_total + jnp.pad(grad_v_piece, pad_rows)
        grad_probs = jnp.einsum(
            "qkgd,tkd->kgqt", grad_block, values[:row_stop], preferred_element_type=jnp.float32
        )
        row_delta = jnp.sum(attn_probs * grad_probs, axis=-1, keepdims=True)
        grad_scores = (attn_probs * (grad_probs - row_delta) * score_scale).astype(jnp.bfloat16)
        grad_q_parts.append(
            jnp.einsum(
                "kgqt,tkd->qkgd", grad_scores, k_rot[:row_stop], preferred_element_type=jnp.float32
            )
        )
        grad_k_piece = jnp.einsum(
            "kgqt,qkgd->tkd",
            grad_scores,
            q_rot[row_start:row_stop],
            preferred_element_type=jnp.float32,
        )
        grad_k_total = grad_k_total + jnp.pad(grad_k_piece, pad_rows)
    return (jnp.concatenate(grad_q_parts, axis=0), grad_k_total, grad_v_total.astype(jnp.bfloat16))


def spread_rows(local_rows):
    return lax.all_gather(local_rows, "tp", axis=0, tiled=True)


def spread_grads(local_rows):
    return lax.all_gather(local_rows, "tp", axis=0, tiled=True)


def branch_sum(left_arg, right_arg, row_total):
    return lax.psum_scatter(
        mat_dot(
            lax.dynamic_slice_in_dim(left_arg, jnp.int32(0), row_total * lax.axis_size("tp"), 0),
            right_arg,
        ).astype(jnp.bfloat16),
        "tp",
        scatter_dimension=0,
        tiled=True,
    ).astype(jnp.float32)


def input_sum(lefts, rights, row_total):
    row_start = jnp.int32(0)
    row_count = row_total * lax.axis_size("tp")
    total_sum = dot_right_t(lax.dynamic_slice_in_dim(lefts[0], row_start, row_count, 0), rights[0])
    for pair_index in range(1, len(lefts)):
        total_sum = total_sum + dot_right_t(
            lax.dynamic_slice_in_dim(lefts[pair_index], row_start, row_count, 0), rights[pair_index]
        )
    return lax.psum_scatter(
        total_sum.astype(jnp.bfloat16), "tp", scatter_dimension=0, tiled=True
    ).astype(jnp.float32)


def layer_forward(resid, segment_ids, cosine, sine_part, weights):
    (
        w_query,
        w_key,
        w_value,
        w_out,
        w_gate,
        w_up,
        w_down,
        attn_gain,
        mlp_gain,
        query_gain,
        key_gain,
    ) = weights
    local_rows = resid.shape[0]
    seq_count, length = segment_ids.shape
    head_dim = query_gain.shape[0]
    q_heads = w_query.shape[1] // head_dim
    kv_heads = w_key.shape[1] // head_dim
    group_size = q_heads // kv_heads
    normed, hat_attn, scale_attn = row_norm(resid, attn_gain)
    attn_rows = spread_rows(normed.astype(jnp.bfloat16))
    token_count = attn_rows.shape[0]
    queries = mat_dot(attn_rows, w_query).reshape(token_count, q_heads, head_dim)
    keys_raw = mat_dot(attn_rows, w_key).reshape(token_count, kv_heads, head_dim)
    values = mat_dot(attn_rows, w_value).astype(jnp.bfloat16)
    query_normed, query_hat, query_scale = row_norm(queries, query_gain)
    key_normed, key_hat, key_scale = row_norm(keys_raw, key_gain)
    q_rot = rope_apply(query_normed, cosine, sine_part).astype(jnp.bfloat16)
    k_rot = rope_apply(key_normed, cosine, sine_part).astype(jnp.bfloat16)
    attended, log_total = lax.map(
        attend_bundle,
        (
            q_rot.reshape(seq_count, length, kv_heads, group_size, head_dim),
            k_rot.reshape(seq_count, length, kv_heads, head_dim),
            values.reshape(seq_count, length, kv_heads, head_dim),
            segment_ids,
        ),
    )
    attended = attended.reshape(token_count, q_heads * head_dim)
    resid_mid = resid + branch_sum(attended, w_out, local_rows)
    normed_mlp, hat_mlp, scale_mlp = row_norm(resid_mid, mlp_gain)
    mlp_rows = spread_rows(normed_mlp.astype(jnp.bfloat16))
    gate_act = mat_dot(mlp_rows, w_gate)
    up_act = mat_dot(mlp_rows, w_up)
    hidden_act = (jax.nn.silu(gate_act) * up_act).astype(jnp.bfloat16)
    resid_next = resid_mid + branch_sum(hidden_act, w_down, local_rows)
    kept_state = (
        hat_attn,
        scale_attn,
        attn_rows,
        query_hat,
        query_scale,
        key_hat,
        key_scale,
        q_rot,
        k_rot,
        values,
        log_total,
        attended,
        hat_mlp,
        scale_mlp,
        mlp_rows,
        gate_act,
        up_act,
        hidden_act,
    )
    return (resid_next, kept_state)


def layer_backward(grad_resid, segment_ids, cosine, sine_part, weights, kept_state):
    (
        w_query,
        w_key,
        w_value,
        w_out,
        w_gate,
        w_up,
        w_down,
        attn_gain,
        mlp_gain,
        query_gain,
        key_gain,
    ) = weights
    (
        hat_attn,
        scale_attn,
        attn_rows,
        query_hat,
        query_scale,
        key_hat,
        key_scale,
        q_rot,
        k_rot,
        values,
        log_total,
        attended,
        hat_mlp,
        scale_mlp,
        mlp_rows,
        gate_act,
        up_act,
        hidden_act,
    ) = kept_state
    local_rows = grad_resid.shape[0]
    seq_count, length = segment_ids.shape
    head_dim = query_gain.shape[0]
    q_heads = w_query.shape[1] // head_dim
    kv_heads = w_key.shape[1] // head_dim
    group_size = q_heads // kv_heads
    token_count = attn_rows.shape[0]
    grad_half = spread_grads(grad_resid.astype(jnp.bfloat16))
    grad_down = dot_left_t(hidden_act, grad_half)
    grad_hidden = dot_right_t(grad_half, w_down)
    sigmoid_gate = jax.nn.sigmoid(gate_act)
    grad_gate_act = (
        grad_hidden * up_act * sigmoid_gate * (1.0 + gate_act * (1.0 - sigmoid_gate))
    ).astype(jnp.bfloat16)
    grad_up_act = (grad_hidden * gate_act * sigmoid_gate).astype(jnp.bfloat16)
    grad_gate = dot_left_t(mlp_rows, grad_gate_act)
    grad_up = dot_left_t(mlp_rows, grad_up_act)
    grad_normed_mlp = input_sum((grad_gate_act, grad_up_act), (w_gate, w_up), local_rows)
    grad_norm_in, grad_mlp_gain = norm_back(grad_normed_mlp, hat_mlp, scale_mlp, mlp_gain, (0,))
    grad_mid = grad_resid + grad_norm_in
    grad_mid_half = spread_grads(grad_mid.astype(jnp.bfloat16))
    grad_out = dot_left_t(attended, grad_mid_half)
    grad_attended = dot_right_t(grad_mid_half, w_out).astype(jnp.bfloat16)
    grad_q_rot, grad_k_rot, grad_values = lax.map(
        back_bundle,
        (
            q_rot.reshape(seq_count, length, kv_heads, group_size, head_dim),
            k_rot.reshape(seq_count, length, kv_heads, head_dim),
            values.reshape(seq_count, length, kv_heads, head_dim),
            segment_ids,
            log_total,
            grad_attended.reshape(seq_count, length, kv_heads, group_size, head_dim),
        ),
    )
    grad_qn = rope_back(grad_q_rot.reshape(token_count, q_heads, head_dim), cosine, sine_part)
    grad_kn = rope_back(grad_k_rot.reshape(token_count, kv_heads, head_dim), cosine, sine_part)
    grad_queries_wide, grad_query_gain = norm_back(
        grad_qn, query_hat, query_scale, query_gain, (0, 1)
    )
    grad_keys_wide, grad_key_gain = norm_back(grad_kn, key_hat, key_scale, key_gain, (0, 1))
    grad_queries = grad_queries_wide.reshape(token_count, q_heads * head_dim).astype(jnp.bfloat16)
    grad_keys = grad_keys_wide.reshape(token_count, kv_heads * head_dim).astype(jnp.bfloat16)
    grad_values = grad_values.reshape(token_count, kv_heads * head_dim)
    grad_query = dot_left_t(attn_rows, grad_queries)
    grad_key = dot_left_t(attn_rows, grad_keys)
    grad_value = dot_left_t(attn_rows, grad_values)
    grad_normed_attn = input_sum(
        (grad_queries, grad_keys, grad_values), (w_query, w_key, w_value), local_rows
    )
    grad_attn_in, grad_attn_gain = norm_back(
        grad_normed_attn, hat_attn, scale_attn, attn_gain, (0,)
    )
    grad_in = grad_mid + grad_attn_in
    return (
        grad_in,
        (
            grad_query,
            grad_key,
            grad_value,
            grad_out,
            grad_gate,
            grad_up,
            grad_down,
            grad_attn_gain,
            grad_mlp_gain,
            grad_query_gain,
            grad_key_gain,
        ),
    )


def local(
    inputs,
    segment_ids,
    attn_norm,
    mlp_norm,
    query_norm,
    key_norm,
    w_query,
    w_key,
    w_value,
    w_out,
    w_gate,
    w_up,
    w_down,
    cotangent,
):
    positions = positions_of(segment_ids)
    cosine, sine_part = rope_tables(positions, HD)
    layer_count = w_query.shape[0]
    resid = inputs
    layers_kept = []
    layers_full = []
    for layer_idx in range(layer_count):
        full_weights = (
            lax.all_gather(w_query[layer_idx], "fsdp", axis=0, tiled=True),
            lax.all_gather(w_key[layer_idx], "fsdp", axis=0, tiled=True),
            lax.all_gather(w_value[layer_idx], "fsdp", axis=0, tiled=True),
            lax.all_gather(w_out[layer_idx], "fsdp", axis=1, tiled=True),
            lax.all_gather(w_gate[layer_idx], "fsdp", axis=0, tiled=True),
            lax.all_gather(w_up[layer_idx], "fsdp", axis=0, tiled=True),
            lax.all_gather(w_down[layer_idx], "fsdp", axis=1, tiled=True),
            lax.all_gather(attn_norm[layer_idx], "fsdp", axis=0, tiled=True),
            lax.all_gather(mlp_norm[layer_idx], "fsdp", axis=0, tiled=True),
            lax.all_gather(query_norm[layer_idx], "fsdp", axis=0, tiled=True),
            lax.all_gather(key_norm[layer_idx], "fsdp", axis=0, tiled=True),
        )
        resid, kept_state = layer_forward(resid, segment_ids, cosine, sine_part, full_weights)
        layers_kept.append(kept_state)
        layers_full.append(full_weights)
    grad_resid = cotangent
    grads_list = []
    for layer_idx in reversed(range(layer_count)):
        full_weights = (
            lax.all_gather(w_query[layer_idx], "fsdp", axis=0, tiled=True),
            lax.all_gather(w_key[layer_idx], "fsdp", axis=0, tiled=True),
            lax.all_gather(w_value[layer_idx], "fsdp", axis=0, tiled=True),
            lax.all_gather(w_out[layer_idx], "fsdp", axis=1, tiled=True),
            lax.all_gather(w_gate[layer_idx], "fsdp", axis=0, tiled=True),
            lax.all_gather(w_up[layer_idx], "fsdp", axis=0, tiled=True),
            lax.all_gather(w_down[layer_idx], "fsdp", axis=1, tiled=True),
            lax.all_gather(attn_norm[layer_idx], "fsdp", axis=0, tiled=True),
            lax.all_gather(mlp_norm[layer_idx], "fsdp", axis=0, tiled=True),
            lax.all_gather(query_norm[layer_idx], "fsdp", axis=0, tiled=True),
            lax.all_gather(key_norm[layer_idx], "fsdp", axis=0, tiled=True),
        )
        grad_resid, grad_parts = layer_backward(
            grad_resid, segment_ids, cosine, sine_part, full_weights, layers_kept[layer_idx]
        )
        gains_summed = lax.psum((grad_parts[7], grad_parts[8], grad_parts[9], grad_parts[10]), "tp")
        grad_parts = tuple(grad_parts[:7]) + tuple(gains_summed)
        grad_parts = (
            lax.psum_scatter(
                grad_parts[0].astype(jnp.bfloat16), "fsdp", scatter_dimension=0, tiled=True
            ).astype(jnp.float32),
            lax.psum_scatter(
                grad_parts[1].astype(jnp.bfloat16), "fsdp", scatter_dimension=0, tiled=True
            ).astype(jnp.float32),
            lax.psum_scatter(
                grad_parts[2].astype(jnp.bfloat16), "fsdp", scatter_dimension=0, tiled=True
            ).astype(jnp.float32),
            lax.psum_scatter(
                grad_parts[3].astype(jnp.bfloat16), "fsdp", scatter_dimension=1, tiled=True
            ).astype(jnp.float32),
            lax.psum_scatter(
                grad_parts[4].astype(jnp.bfloat16), "fsdp", scatter_dimension=0, tiled=True
            ).astype(jnp.float32),
            lax.psum_scatter(
                grad_parts[5].astype(jnp.bfloat16), "fsdp", scatter_dimension=0, tiled=True
            ).astype(jnp.float32),
            lax.psum_scatter(
                grad_parts[6].astype(jnp.bfloat16), "fsdp", scatter_dimension=1, tiled=True
            ).astype(jnp.float32),
            lax.psum_scatter(
                grad_parts[7].astype(jnp.bfloat16), "fsdp", scatter_dimension=0, tiled=True
            ).astype(jnp.float32),
            lax.psum_scatter(
                grad_parts[8].astype(jnp.bfloat16), "fsdp", scatter_dimension=0, tiled=True
            ).astype(jnp.float32),
            lax.psum_scatter(
                grad_parts[9].astype(jnp.bfloat16), "fsdp", scatter_dimension=0, tiled=True
            ).astype(jnp.float32),
            lax.psum_scatter(
                grad_parts[10].astype(jnp.bfloat16), "fsdp", scatter_dimension=0, tiled=True
            ).astype(jnp.float32),
        )
        grads_list.insert(0, grad_parts)
    stacked = tuple(
        (
            jnp.stack([grads_list[layer_idx][slot_index] for layer_idx in range(layer_count)])
            for slot_index in range(11)
        )
    )
    return (
        resid,
        grad_resid,
        stacked[0],
        stacked[1],
        stacked[2],
        stacked[3],
        stacked[4],
        stacked[5],
        stacked[6],
        stacked[7],
        stacked[8],
        stacked[9],
        stacked[10],
    )


def solution(mesh):
    return jax.shard_map(
        local,
        mesh=mesh,
        in_specs=(
            P(("fsdp", "tp"), None),
            P("fsdp", None),
            P(None, "fsdp"),
            P(None, "fsdp"),
            P(None, "fsdp"),
            P(None, "fsdp"),
            P(None, "fsdp", "tp"),
            P(None, "fsdp", "tp"),
            P(None, "fsdp", "tp"),
            P(None, "tp", "fsdp"),
            P(None, "fsdp", "tp"),
            P(None, "fsdp", "tp"),
            P(None, "tp", "fsdp"),
            P(("fsdp", "tp"), None),
        ),
        out_specs=(
            P(("fsdp", "tp"), None),
            P(("fsdp", "tp"), None),
            P(None, "fsdp", "tp"),
            P(None, "fsdp", "tp"),
            P(None, "fsdp", "tp"),
            P(None, "tp", "fsdp"),
            P(None, "fsdp", "tp"),
            P(None, "fsdp", "tp"),
            P(None, "tp", "fsdp"),
            P(None, "fsdp"),
            P(None, "fsdp"),
            P(None, "fsdp"),
            P(None, "fsdp"),
        ),
        check_vma=False,
    )
```

profile of v0, /device:TPU:0, one launch (start us, length us, event | category | flops | bytes accessed | tf_op | source)
XLA Modules:
  0.0 1541.5 jit_solution(5576441074346377639)
XLA Ops:
  9.5 13.4 all-gather
  29.2 14.5 all-reduce.18
  47.0 15.9 %all-gather.1 = bf16[1,1024,256]{2,1,0:T(8,128)(2,1)} all-gather(bf16[1,128,256]{2,1,0:T(8,128)(2,1)S(1)} %get-tuple-element.206), channel_id=3, replica_groups=mesh['fsdp'=8,'tp'=4] {'fsdp'}, dimensions={1}, use_global_device_ids=true | all-gather | bytes 589824 | tf_op jit(solution)/shard_map/all_gather | solution.py:412
  62.8 17.3 %all-gather.2 = bf16[1,1024,256]{2,1,0:T(8,128)(2,1)S(1)} all-gather(bf16[1,128,256]{2,1,0:T(8,128)(2,1)S(1)} %get-tuple-element.204), channel_id=4, replica_groups=mesh['fsdp'=8,'tp'=4] {'fsdp'}, dimensions={1}, use_global_device_ids=true | all-gather | bytes 589824 | tf_op jit(solution)/shard_map/all_gather | solution.py:411
  92.7 5.7 fusion.31
  103.8 9.9 fusion.11
  125.2 10.3 all-gather.7
  135.4 22.4 %reduce-scatter.31.cloned.1.call-done = bf16[256,1024]{1,0:T(8,128)(2,1)} async-done(((bf16[1024,1024]{1,0:T(8,128)(2,1)}), bf16[256,1024]{1,0:T(8,128)(2,1)}) %reduce-scatter.31.cloned.1.call-update) | async-done | bytes 524304 | tf_op jit(solution)/shard_map/reduce_scatter | solution.py:187
  163.0 21.6 %all-gather.61.cloned.1.call-done = bf16[1,1024,768]{2,1,0:T(8,128)(2,1)} async-done(((bf16[1,128,768]{2,1,0:T(8,128)(2,1)}), bf16[1,1024,768]{2,1,0:T(8,128)(2,1)}) %all-gather.61.cloned.1.call-update) | async-done | bytes 1572880 | tf_op jit(solution)/shard_map/all_gather | solution.py:414
  184.6 36.6 %all-gather.43.cloned.1.call-done = bf16[1024,1024]{1,0:T(8,128)(2,1)} async-done(((bf16[256,1024]{1,0:T(8,128)(2,1)}), bf16[1024,1024]{1,0:T(8,128)(2,1)}) %all-gather.43.cloned.1.call-update) | async-done | bytes 2097168 | tf_op jit(solution)/shard_map/all_gather | solution.py:179
  221.2 5.6 fusion.105
  226.8 21.3 %all-gather.63.cloned.1.call-done = bf16[1,1024,768]{2,1,0:T(8,128)(2,1)} async-done(((bf16[1,128,768]{2,1,0:T(8,128)(2,1)}), bf16[1,1024,768]{2,1,0:T(8,128)(2,1)}) %all-gather.63.cloned.1.call-update) | async-done | bytes 1572880 | tf_op jit(solution)/shard_map/all_gather | solution.py:415
  248.2 7.1 multiply_convert_fusion.5
  255.3 20.7 %all-gather.65.cloned.1.call-done = bf16[1,768,1024]{2,1,0:T(8,128)(2,1)} async-done(((bf16[1,768,128]{2,1,0:T(8,128)(2,1)}), bf16[1,768,1024]{2,1,0:T(8,128)(2,1)}) %all-gather.65.cloned.1.call-update) | async-done | bytes 1572880 | tf_op jit(solution)/shard_map/all_gather | solution.py:416
  281.1 11.6 all-gather.11
  292.7 22.5 %reduce-scatter.33.cloned.1.call-done = bf16[256,1024]{1,0:T(8,128)(2,1)} async-done(((bf16[1024,1024]{1,0:T(8,128)(2,1)}), bf16[256,1024]{1,0:T(8,128)(2,1)}) %reduce-scatter.33.cloned.1.call-update) | async-done | bytes 524304 | tf_op jit(solution)/shard_map/reduce_scatter | solution.py:187
  321.3 15.8 %all-gather.12 = bf16[1,1024,256]{2,1,0:T(8,128)(2,1)} all-gather(bf16[1,128,256]{2,1,0:T(8,128)(2,1)S(1)} %get-tuple-element.205), channel_id=14, replica_groups=mesh['fsdp'=8,'tp'=4] {'fsdp'}, dimensions={1}, use_global_device_ids=true | all-gather | bytes 589824 | tf_op jit(solution)/shard_map/all_gather | solution.py:412
  337.1 16.0 %all-gather.13 = bf16[1,1024,256]{2,1,0:T(8,128)(2,1)} all-gather(bf16[1,128,256]{2,1,0:T(8,128)(2,1)S(1)} %get-tuple-element.203), channel_id=15, replica_groups=mesh['fsdp'=8,'tp'=4] {'fsdp'}, dimensions={1}, use_global_device_ids=true | all-gather | bytes 589824 | tf_op jit(solution)/shard_map/all_gather | solution.py:411
  362.2 14.6 all-gather.67.cloned.1.call-done
  383.3 6.0 fusion.29
  395.5 10.9 fusion.9
  416.6 10.5 all-gather.18
  427.1 23.7 %reduce-scatter.35.cloned.1.call-done = bf16[256,1024]{1,0:T(8,128)(2,1)} async-done(((bf16[1024,1024]{1,0:T(8,128)(2,1)}), bf16[256,1024]{1,0:T(8,128)(2,1)}) %reduce-scatter.35.cloned.1.call-update) | async-done | bytes 524304 | tf_op jit(solution)/shard_map/reduce_scatter | solution.py:187
  457.5 20.0 %all-gather.73.cloned.1.call-done = bf16[1,1024,768]{2,1,0:T(8,128)(2,1)} async-done(((bf16[1,128,768]{2,1,0:T(8,128)(2,1)}), bf16[1,1024,768]{2,1,0:T(8,128)(2,1)}) %all-gather.73.cloned.1.call-update) | async-done | bytes 1572880 | tf_op jit(solution)/shard_map/all_gather | solution.py:415
  477.6 36.6 %all-gather.47.cloned.1.call-done = bf16[1024,1024]{1,0:T(8,128)(2,1)} async-done(((bf16[256,1024]{1,0:T(8,128)(2,1)}), bf16[1024,1024]{1,0:T(8,128)(2,1)}) %all-gather.47.cloned.1.call-update) | async-done | bytes 2097168 | tf_op jit(solution)/shard_map/all_gather | solution.py:179
  514.2 5.5 fusion.91
  519.7 21.3 %all-gather.71.cloned.1.call-done = bf16[1,1024,768]{2,1,0:T(8,128)(2,1)} async-done(((bf16[1,128,768]{2,1,0:T(8,128)(2,1)}), bf16[1,1024,768]{2,1,0:T(8,128)(2,1)}) %all-gather.71.cloned.1.call-update) | async-done | bytes 1572880 | tf_op jit(solution)/shard_map/all_gather | solution.py:414
  541.0 5.4 fusion.95
  546.4 22.2 %all-gather.75.cloned.1.call-done = bf16[1,768,1024]{2,1,0:T(8,128)(2,1)} async-done(((bf16[1,768,128]{2,1,0:T(8,128)(2,1)}), bf16[1,768,1024]{2,1,0:T(8,128)(2,1)}) %all-gather.75.cloned.1.call-update) | async-done | bytes 1572880 | tf_op jit(solution)/shard_map/all_gather | solution.py:416
  568.7 35.7 %all-gather.49.cloned.1.call-done = bf16[1024,1024]{1,0:T(8,128)(2,1)} async-done(((bf16[256,1024]{1,0:T(8,128)(2,1)}), bf16[1024,1024]{1,0:T(8,128)(2,1)}) %all-gather.49.cloned.1.call-update) | async-done | bytes 2097168 | tf_op jit(solution)/shard_map/all_gather | solution.py:183
  604.4 8.0 multiply_convert_fusion.2
  618.2 35.3 %reduce-scatter.39.cloned.1.call-done = bf16[256,1024]{1,0:T(8,128)(2,1)} async-done(((bf16[1024,1024]{1,0:T(8,128)(2,1)}), bf16[256,1024]{1,0:T(8,128)(2,1)}) %reduce-scatter.39.cloned.1.call-update) | async-done | bytes 524304 | tf_op jit(solution)/shard_map/reduce_scatter | solution.py:206
  656.6 35.1 %all-gather.51.cloned.1.call-done = bf16[1024,1024]{1,0:T(8,128)(2,1)} async-done(((bf16[256,1024]{1,0:T(8,128)(2,1)}), bf16[1024,1024]{1,0:T(8,128)(2,1)}) %all-gather.51.cloned.1.call-update) | async-done | bytes 2097168 | tf_op jit(solution)/shard_map/all_gather | solution.py:183
  700.3 8.5 fusion.156
  708.8 9.0 fusion.120
  717.8 5.9 fusion.276
  732.2 14.4 fusion.116
  746.7 15.2 fusion.118
  787.4 30.2 %reduce-scatter.41.cloned.1.call-done = bf16[256,1024]{1,0:T(8,128)(2,1)} async-done(((bf16[1024,1024]{1,0:T(8,128)(2,1)}), bf16[256,1024]{1,0:T(8,128)(2,1)}) %reduce-scatter.41.cloned.1.call-update) | async-done | bytes 524304 | tf_op jit(solution)/shard_map/reduce_scatter | solution.py:206
  819.1 36.7 %reduce-scatter.37.cloned.1.call-done = bf16[256,1024]{1,0:T(8,128)(2,1)} async-done(((bf16[1024,1024]{1,0:T(8,128)(2,1)}), bf16[256,1024]{1,0:T(8,128)(2,1)}) %reduce-scatter.37.cloned.1.call-update) | async-done | bytes 524304 | tf_op jit(solution)/shard_map/reduce_scatter | solution.py:187
  860.1 34.9 %all-gather.53.cloned.1.call-done = bf16[1024,1024]{1,0:T(8,128)(2,1)} async-done(((bf16[256,1024]{1,0:T(8,128)(2,1)}), bf16[1024,1024]{1,0:T(8,128)(2,1)}) %all-gather.53.cloned.1.call-update) | async-done | bytes 2097168 | tf_op jit(solution)/shard_map/all_gather | solution.py:183
  895.0 6.6 multiply_convert_fusion
  907.4 35.3 %reduce-scatter.43.cloned.1.call-done = bf16[256,1024]{1,0:T(8,128)(2,1)} async-done(((bf16[1024,1024]{1,0:T(8,128)(2,1)}), bf16[256,1024]{1,0:T(8,128)(2,1)}) %reduce-scatter.43.cloned.1.call-update) | async-done | bytes 524304 | tf_op jit(solution)/shard_map/reduce_scatter | solution.py:206
  945.6 5.1 convolution_convert_fusion.4
  983.2 5.2 convolution_convert_fusion.9
  996.0 5.1 fusion.133
  1015.7 8.2 fusion.155
  1023.9 14.9 fusion.115
  1059.8 7.9 fusion.119
  1067.7 14.6 fusion.113
  1101.9 17.9 %reduce-scatter.65.cloned.1.call-done = bf16[128,768]{1,0:T(8,128)(2,1)} async-done(((bf16[1024,768]{1,0:T(8,128)(2,1)}), bf16[128,768]{1,0:T(8,128)(2,1)}) %reduce-scatter.65.cloned.1.call-update) | async-done | bytes 196624 | tf_op jit(solution)/shard_map/reduce_scatter | solution.py:462
  1119.8 34.7 %reduce-scatter.63.cloned.1.call-done = bf16[128,768]{1,0:T(8,128)(2,1)} async-done(((bf16[1024,768]{1,0:T(8,128)(2,1)}), bf16[128,768]{1,0:T(8,128)(2,1)}) %reduce-scatter.63.cloned.1.call-update) | async-done | bytes 196624 | tf_op jit(solution)/shard_map/reduce_scatter | solution.py:462
  1156.5 32.9 %reduce-scatter.61.cloned.1.call-done = bf16[128,768]{1,0:T(8,128)(2,1)} async-done(((bf16[1024,768]{1,0:T(8,128)(2,1)}), bf16[128,768]{1,0:T(8,128)(2,1)}) %reduce-scatter.61.cloned.1.call-update) | async-done | bytes 196624 | tf_op jit(solution)/shard_map/reduce_scatter | solution.py:459
  1189.4 35.0 %reduce-scatter.59.cloned.1.call-done = bf16[128,768]{1,0:T(8,128)(2,1)} async-done(((bf16[1024,768]{1,0:T(8,128)(2,1)}), bf16[128,768]{1,0:T(8,128)(2,1)}) %reduce-scatter.59.cloned.1.call-update) | async-done | bytes 196624 | tf_op jit(solution)/shard_map/reduce_scatter | solution.py:459
  1226.3 29.7 %reduce-scatter.57.cloned.1.call-done = bf16[128,256]{1,0:T(8,128)(2,1)} async-done(((bf16[1024,256]{1,0:T(8,128)(2,1)}), bf16[128,256]{1,0:T(8,128)(2,1)}) %reduce-scatter.57.cloned.1.call-update) | async-done | bytes 65552 | tf_op jit(solution)/shard_map/reduce_scatter | solution.py:453
  1256.0 31.7 %reduce-scatter.55.cloned.1.call-done = bf16[128,256]{1,0:T(8,128)(2,1)} async-done(((bf16[1024,256]{1,0:T(8,128)(2,1)}), bf16[128,256]{1,0:T(8,128)(2,1)}) %reduce-scatter.55.cloned.1.call-update) | async-done | bytes 65552 | tf_op jit(solution)/shard_map/reduce_scatter | solution.py:453
  1289.4 30.2 %reduce-scatter.53.cloned.1.call-done = bf16[128,256]{1,0:T(8,128)(2,1)} async-done(((bf16[1024,256]{1,0:T(8,128)(2,1)}), bf16[128,256]{1,0:T(8,128)(2,1)}) %reduce-scatter.53.cloned.1.call-update) | async-done | bytes 65552 | tf_op jit(solution)/shard_map/reduce_scatter | solution.py:450
  1319.6 31.5 %reduce-scatter.51.cloned.1.call-done = bf16[128,256]{1,0:T(8,128)(2,1)} async-done(((bf16[1024,256]{1,0:T(8,128)(2,1)}), bf16[128,256]{1,0:T(8,128)(2,1)}) %reduce-scatter.51.cloned.1.call-update) | async-done | bytes 65552 | tf_op jit(solution)/shard_map/reduce_scatter | solution.py:450
  1352.7 31.3 %reduce-scatter.67.cloned.1.call-done = bf16[128,512]{1,0:T(8,128)(2,1)} async-done(((bf16[1024,512]{1,0:T(8,128)(2,1)}), bf16[128,512]{1,0:T(8,128)(2,1)}) %reduce-scatter.67.cloned.1.call-update) | async-done | bytes 131088
  1385.9 31.2 %reduce-scatter.49.cloned.1.call-done = bf16[128,512]{1,0:T(8,128)(2,1)} async-done(((bf16[1024,512]{1,0:T(8,128)(2,1)}), bf16[128,512]{1,0:T(8,128)(2,1)}) %reduce-scatter.49.cloned.1.call-update) | async-done | bytes 131088 | tf_op jit(solution)/shard_map/reduce_scatter | solution.py:447
  1417.1 32.9 %reduce-scatter.47.cloned.1.call-done = bf16[128,512]{1,0:T(8,128)(2,1)} async-done(((bf16[1024,512]{1,0:T(8,128)(2,1)}), bf16[128,512]{1,0:T(8,128)(2,1)}) %reduce-scatter.47.cloned.1.call-update) | async-done | bytes 131088 | tf_op jit(solution)/shard_map/reduce_scatter | solution.py:447
  1451.8 34.6 %reduce-scatter.45.cloned.1.call-done = bf16[256,1024]{1,0:T(8,128)(2,1)} async-done(((bf16[1024,1024]{1,0:T(8,128)(2,1)}), bf16[256,1024]{1,0:T(8,128)(2,1)}) %reduce-scatter.45.cloned.1.call-update) | async-done | bytes 524304 | tf_op jit(solution)/shard_map/reduce_scatter | solution.py:206
  1487.9 15.4 %all-reduce.16 = (bf16[1024]{0:T(1024)(128)(2,1)S(1)}, bf16[1024]{0:T(1024)(128)(2,1)S(1)}, bf16[1024]{0:T(1024)(128)(2,1)S(1)}, bf16[1024]{0:T(1024)(128)(2,1)S...) all-reduce(f32[1024]{0:T(1024)S(1)} %get-tuple-element.101, ...), channel_id=1, replica_groups=mesh['fsdp'=8,'tp'=4] {'tp'}, use_global_device_ids=true, to_apply=%region_52.53 | all-reduce | flops 4608 | bytes 27648 | tf_op jit(solution)/shard_map/psum | solution.py:444
  1503.4 25.9 %all-reduce.17 = (bf16[1024]{0:T(1024)(128)(2,1)S(1)}, bf16[1024]{0:T(1024)(128)(2,1)S(1)}, bf16[1024]{0:T(1024)(128)(2,1)S(1)}, bf16[1024]{0:T(1024)(128)(2,1)S...) all-reduce(bf16[1024]{0:T(1024)(128)(2,1)S(1)} %get-tuple-element.1, ...), channel_id=47, replica_groups=mesh['fsdp'=8,'tp'=4] {'fsdp'}, use_global_device_ids=true, to_apply=%region_53.54.clone | all-reduce | flops 4608 | bytes 18432
  (494 shorter events, 271.4 us)
Async XLA Ops:
  7.2 19.9 %copy-start.96 = (u32[32]{0:T(128)S(1)}, u32[32]{0:T(128)}, u32[]{:S(2)}) copy-start(u32[32]{0:T(128)} %constant.148) | copy-start | bytes 388
  7.2 18.1 %copy-start.79 = (bf16[2,128,512]{2,1,0:T(8,128)(2,1)S(1)}, bf16[2,128,512]{2,1,0:T(8,128)(2,1)}, u32[]{:S(2)}) copy-start(bf16[2,128,512]{2,1,0:T(8,128)(2,1)} %param.20) | copy-start | bytes 786436
  7.2 18.9 %copy-start.80 = (bf16[2,512,128]{2,1,0:T(8,128)(2,1)S(1)}, bf16[2,512,128]{2,1,0:T(8,128)(2,1)}, u32[]{:S(2)}) copy-start(bf16[2,512,128]{2,1,0:T(8,128)(2,1)} %param.23) | copy-start | bytes 786436
  7.2 19.7 %copy-start.85 = (s32[1,1024]{1,0:T(1,128)S(1)}, s32[1,1024]{1,0:T(1,128)}, u32[]{:S(2)}) copy-start(s32[1,1024]{1,0:T(1,128)} %param.15) | copy-start | bytes 12292
  7.2 19.8 %copy-start.97 = (bf16[2,16]{1,0:T(2,128)(2,1)S(1)}, bf16[2,16]{1,0:T(2,128)(2,1)}, u32[]{:S(2)}) copy-start(bf16[2,16]{1,0:T(2,128)(2,1)} %param.18) | copy-start | bytes 196
  7.2 19.8 %copy-start.98 = (bf16[2,16]{1,0:T(2,128)(2,1)S(1)}, bf16[2,16]{1,0:T(2,128)(2,1)}, u32[]{:S(2)}) copy-start(bf16[2,16]{1,0:T(2,128)(2,1)} %param.19) | copy-start | bytes 196
  7.2 37.3 %copy-start.83 = (bf16[2,128,256]{2,1,0:T(8,128)(2,1)S(1)}, bf16[2,128,256]{2,1,0:T(8,128)(2,1)}, u32[]{:S(2)}) copy-start(bf16[2,128,256]{2,1,0:T(8,128)(2,1)} %param.21) | copy-start | bytes 393220
  7.3 74.1 %all-gather.41.cloned.1.call-start = ((), (), s32[]{:S(2)}) async-start(), calls=%async_computation.22 | async-start | bytes 2621440 | tf_op jit(solution)/shard_map/all_gather | solution.py:179
  8.8 35.8 %copy-start.84 = (bf16[2,128,256]{2,1,0:T(8,128)(2,1)S(1)}, bf16[2,128,256]{2,1,0:T(8,128)(2,1)}, u32[]{:S(2)}) copy-start(bf16[2,128,256]{2,1,0:T(8,128)(2,1)} %param.22) | copy-start | bytes 393220
  8.8 18.1 %copy-start.88 = (f32[256]{0:T(256)}, f32[256]{0:T(256)S(1)}, u32[]{:S(2)}) copy-start(f32[256]{0:T(256)S(1)} %add_rsqrt_fusion.7) | copy-start | bytes 3076
  23.0 22.5 %copy-start.86 = (f32[1,1024]{1,0:T(1,128)}, f32[1,1024]{1,0:T(1,128)S(1)}, u32[]{:S(2)}) copy-start(f32[1,1024]{1,0:T(1,128)S(1)} %convert_element_type.415) | copy-start | bytes 12292
  25.2 60.2 %all-gather.57.cloned.1.call-start = ((), (), s32[]{:S(2)}) async-start(), calls=%async_computation.48 | async-start | bytes 1179648 | tf_op jit(solution)/shard_map/all_gather | solution.py:410
  26.0 92.0 %all-gather.59.cloned.1.call-start = ((), (), s32[]{:S(2)}) async-start(), calls=%async_computation.49 | async-start | bytes 1179648 | tf_op jit(solution)/shard_map/all_gather | solution.py:413
  26.8 131.0 %reduce-scatter.31.cloned.1.call-start = ((), (), s32[]{:S(2)}) async-start(), calls=%async_computation.23 | async-start | bytes 2621440 | tf_op jit(solution)/shard_map/reduce_scatter | solution.py:187
  43.7 44.9 %copy-start.90 = (f32[128]{0:T(128)}, f32[128]{0:T(128)S(1)}, u32[]{:S(2)}) copy-start(f32[128]{0:T(128)S(1)} %convert_element_type.424) | copy-start | bytes 1540
  43.7 47.5 %copy-start.93 = (f32[128]{0:T(128)}, f32[128]{0:T(128)S(1)}, u32[]{:S(2)}) copy-start(f32[128]{0:T(128)S(1)} %convert_element_type.423) | copy-start | bytes 1540
  46.5 42.5 %copy-start.18 = (f32[1024,64]{0,1:T(8,128)}, f32[1024,64]{0,1:T(8,128)S(1)}, u32[]{:S(2)}) copy-start(f32[1024,64]{0,1:T(8,128)S(1)} %get-tuple-element.208) | copy-start | bytes 786436
  46.7 314.0 %copy-start.11 = (f32[1024,64]{1,0:T(8,128)}, f32[1024,64]{1,0:T(8,128)S(1)}, u32[]{:S(2)}) copy-start(f32[1024,64]{1,0:T(8,128)S(1)} %copy.217) | copy-start | bytes 786436
  47.0 44.7 %copy-start.14 = (f32[1024,64]{1,0:T(8,128)}, f32[1024,64]{1,0:T(8,128)S(1)}, u32[]{:S(2)}) copy-start(f32[1024,64]{1,0:T(8,128)S(1)} %copy.218) | copy-start | bytes 786436
  122.8 35.1 %copy-start = (f32[256,1024]{1,0:T(8,128)S(1)}, f32[256,1024]{1,0:T(8,128)}, u32[]{:S(2)}) copy-start(f32[256,1024]{1,0:T(8,128)} %param.14) | copy-start | bytes 3145732
  122.8 61.8 %all-gather.61.cloned.1.call-start = ((), (), s32[]{:S(2)}) async-start(), calls=%async_computation.50 | async-start | bytes 1769472 | tf_op jit(solution)/shard_map/all_gather | solution.py:414
  124.6 96.7 %all-gather.43.cloned.1.call-start = ((), (), s32[]{:S(2)}) async-start(), calls=%async_computation.24 | async-start | bytes 2621440 | tf_op jit(solution)/shard_map/all_gather | solution.py:179
  135.4 25.8 %copy-start.75 = (bf16[2,128,768]{2,1,0:T(8,128)(2,1)S(1)}, bf16[2,128,768]{2,1,0:T(8,128)(2,1)}, u32[]{:S(2)}) copy-start(bf16[2,128,768]{2,1,0:T(8,128)(2,1)} %param.25) | copy-start | bytes 1179652
  161.2 87.0 %all-gather.63.cloned.1.call-start = ((), (), s32[]{:S(2)}) async-start(), calls=%async_computation.51 | async-start | bytes 1769472 | tf_op jit(solution)/shard_map/all_gather | solution.py:415
  162.1 113.9 %all-gather.65.cloned.1.call-start = ((), (), s32[]{:S(2)}) async-start(), calls=%async_computation.52 | async-start | bytes 1769472 | tf_op jit(solution)/shard_map/all_gather | solution.py:416
  162.9 152.3 %reduce-scatter.33.cloned.1.call-start = ((), (), s32[]{:S(2)}) async-start(), calls=%async_computation.25 | async-start | bytes 2621440 | tf_op jit(solution)/shard_map/reduce_scatter | solution.py:187
  281.1 34.2 %copy-start.6 = (bf16[256,1024]{1,0:T(8,128)(2,1)S(1)}, bf16[256,1024]{1,0:T(8,128)(2,1)}, u32[]{:S(2)}) copy-start(bf16[256,1024]{1,0:T(8,128)(2,1)} %reduce-scatter.31.cloned.1.call-done) | copy-start | bytes 1572868
  281.1 72.0 %all-gather.45.cloned.1.call-start = ((), (), s32[]{:S(2)}) async-start(), calls=%async_computation.26 | async-start | bytes 2621440 | tf_op jit(solution)/shard_map/all_gather | solution.py:179
  317.5 59.2 %all-gather.67.cloned.1.call-start = ((), (), s32[]{:S(2)}) async-start(), calls=%async_computation.53 | async-start | bytes 1179648 | tf_op jit(solution)/shard_map/all_gather | solution.py:410
  318.3 93.4 %all-gather.69.cloned.1.call-start = ((), (), s32[]{:S(2)}) async-start(), calls=%async_computation.54 | async-start | bytes 1179648 | tf_op jit(solution)/shard_map/all_gather | solution.py:413
  318.8 132.0 %reduce-scatter.35.cloned.1.call-start = ((), (), s32[]{:S(2)}) async-start(), calls=%async_computation.27 | async-start | bytes 2621440 | tf_op jit(solution)/shard_map/reduce_scatter | solution.py:187
  362.2 17.8 %copy-start.92 = (f32[128]{0:T(128)S(1)}, f32[128]{0:T(128)}, u32[]{:S(2)}) copy-start(f32[128]{0:T(128)} %convert_element_type.426) | copy-start | bytes 1540
  415.9 61.7 %all-gather.73.cloned.1.call-start = ((), (), s32[]{:S(2)}) async-start(), calls=%async_computation.56 | async-start | bytes 1769472 | tf_op jit(solution)/shard_map/all_gather | solution.py:415
  416.5 97.7 %all-gather.47.cloned.1.call-start = ((), (), s32[]{:S(2)}) async-start(), calls=%async_computation.28 | async-start | bytes 2621440 | tf_op jit(solution)/shard_map/all_gather | solution.py:179
  454.1 86.9 %all-gather.71.cloned.1.call-start = ((), (), s32[]{:S(2)}) async-start(), calls=%async_computation.55 | async-start | bytes 1769472 | tf_op jit(solution)/shard_map/all_gather | solution.py:414
  454.7 114.0 %all-gather.75.cloned.1.call-start = ((), (), s32[]{:S(2)}) async-start(), calls=%async_computation.57 | async-start | bytes 1769472 | tf_op jit(solution)/shard_map/all_gather | solution.py:416
  455.3 149.1 %all-gather.49.cloned.1.call-start = ((), (), s32[]{:S(2)}) async-start(), calls=%async_computation.30 | async-start | bytes 2621440 | tf_op jit(solution)/shard_map/all_gather | solution.py:183
  457.5 196.0 %reduce-scatter.39.cloned.1.call-start = ((), (), s32[]{:S(2)}) async-start(), calls=%async_computation.31 | async-start | bytes 2621440 | tf_op jit(solution)/shard_map/reduce_scatter | solution.py:206
  618.1 35.4 %copy-start.10 = (bf16[256,1024]{1,0:T(8,128)(2,1)S(1)}, bf16[256,1024]{1,0:T(8,128)(2,1)}, u32[]{:S(2)}) copy-start(bf16[256,1024]{1,0:T(8,128)(2,1)} %reduce-scatter.35.cloned.1.call-done) | copy-start | bytes 1572868
  618.1 73.6 %all-gather.51.cloned.1.call-start = ((), (), s32[]{:S(2)}) async-start(), calls=%async_computation.32 | async-start | bytes 2621440 | tf_op jit(solution)/shard_map/all_gather | solution.py:183
  656.4 161.3 %reduce-scatter.41.cloned.1.call-start = ((), (), s32[]{:S(2)}) async-start(), calls=%async_computation.33 | async-start | bytes 2621440 | tf_op jit(solution)/shard_map/reduce_scatter | solution.py:206
  782.3 73.5 %reduce-scatter.37.cloned.1.call-start = ((), (), s32[]{:S(2)}) async-start(), calls=%async_computation.29 | async-start | bytes 2621440 | tf_op jit(solution)/shard_map/reduce_scatter | solution.py:187
  787.4 107.6 %all-gather.53.cloned.1.call-start = ((), (), s32[]{:S(2)}) async-start(), calls=%async_computation.34 | async-start | bytes 2621440 | tf_op jit(solution)/shard_map/all_gather | solution.py:183
  859.7 83.0 %reduce-scatter.43.cloned.1.call-start = ((), (), s32[]{:S(2)}) async-start(), calls=%async_computation.35 | async-start | bytes 2621440 | tf_op jit(solution)/shard_map/reduce_scatter | solution.py:206
  907.3 37.0 %copy-start.28 = (f32[256,1024]{1,0:T(8,128)S(1)}, f32[256,1024]{1,0:T(8,128)}, u32[]{:S(2)}) copy-start(f32[256,1024]{1,0:T(8,128)} %get-tuple-element.146) | copy-start | bytes 3145732
  907.4 84.4 %all-gather.55.cloned.1.call-start = ((), (), s32[]{:S(2)}) async-start(), calls=%async_computation.36 | async-start | bytes 2621440 | tf_op jit(solution)/shard_map/all_gather | solution.py:183
  945.5 152.2 %reduce-scatter.73.cloned.1.call-start = ((), (), s32[]{:S(2)}) async-start(), calls=%async_computation.61 | async-start | bytes 1769472
  953.4 145.4 %reduce-scatter.69.cloned.1.call-start = ((), (), s32[]{:S(2)}) async-start(), calls=%async_computation.59 | async-start | bytes 1179648
  959.8 140.2 %reduce-scatter.71.cloned.1.call-start = ((), (), s32[]{:S(2)}) async-start(), calls=%async_computation.60 | async-start | bytes 1769472
  967.6 152.3 %reduce-scatter.65.cloned.1.call-start = ((), (), s32[]{:S(2)}) async-start(), calls=%async_computation.47 | async-start | bytes 1769472 | tf_op jit(solution)/shard_map/reduce_scatter | solution.py:462
  972.9 181.6 %reduce-scatter.63.cloned.1.call-start = ((), (), s32[]{:S(2)}) async-start(), calls=%async_computation.46 | async-start | bytes 1769472 | tf_op jit(solution)/shard_map/reduce_scatter | solution.py:462
  978.0 211.4 %reduce-scatter.61.cloned.1.call-start = ((), (), s32[]{:S(2)}) async-start(), calls=%async_computation.45 | async-start | bytes 1769472 | tf_op jit(solution)/shard_map/reduce_scatter | solution.py:459
  983.1 241.2 %reduce-scatter.59.cloned.1.call-start = ((), (), s32[]{:S(2)}) async-start(), calls=%async_computation.44 | async-start | bytes 1769472 | tf_op jit(solution)/shard_map/reduce_scatter | solution.py:459
  988.4 267.6 %reduce-scatter.57.cloned.1.call-start = ((), (), s32[]{:S(2)}) async-start(), calls=%async_computation.43 | async-start | bytes 589824 | tf_op jit(solution)/shard_map/reduce_scatter | solution.py:453
  991.7 296.1 %reduce-scatter.55.cloned.1.call-start = ((), (), s32[]{:S(2)}) async-start(), calls=%async_computation.42 | async-start | bytes 589824 | tf_op jit(solution)/shard_map/reduce_scatter | solution.py:453
  1003.5 316.1 %reduce-scatter.53.cloned.1.call-start = ((), (), s32[]{:S(2)}) async-start(), calls=%async_computation.41 | async-start | bytes 589824 | tf_op jit(solution)/shard_map/reduce_scatter | solution.py:450
  1006.9 344.2 %reduce-scatter.51.cloned.1.call-start = ((), (), s32[]{:S(2)}) async-start(), calls=%async_computation.40 | async-start | bytes 589824 | tf_op jit(solution)/shard_map/reduce_scatter | solution.py:450
  1049.1 334.9 %reduce-scatter.67.cloned.1.call-start = ((), (), s32[]{:S(2)}) async-start(), calls=%async_computation.58 | async-start | bytes 1179648
  1055.5 361.6 %reduce-scatter.49.cloned.1.call-start = ((), (), s32[]{:S(2)}) async-start(), calls=%async_computation.39 | async-start | bytes 1179648 | tf_op jit(solution)/shard_map/reduce_scatter | solution.py:447
  1059.6 390.5 %reduce-scatter.47.cloned.1.call-start = ((), (), s32[]{:S(2)}) async-start(), calls=%async_computation.38 | async-start | bytes 1179648 | tf_op jit(solution)/shard_map/reduce_scatter | solution.py:447
  1090.2 396.3 %reduce-scatter.45.cloned.1.call-start = ((), (), s32[]{:S(2)}) async-start(), calls=%async_computation.37 | async-start | bytes 2621440 | tf_op jit(solution)/shard_map/reduce_scatter | solution.py:206
  1156.5 330.0 %copy-start.87 = (f32[1,1024]{1,0:T(1,128)S(1)}, f32[1,1024]{1,0:T(1,128)}, u32[]{:S(2)}) copy-start(f32[1,1024]{1,0:T(1,128)} %copy-done.86) | copy-start | bytes 12292
  1156.5 330.0 %copy-start.89 = (f32[256]{0:T(256)S(1)}, f32[256]{0:T(256)}, u32[]{:S(2)}) copy-start(f32[256]{0:T(256)} %copy-done.88) | copy-start | bytes 3076
  1287.8 244.2 %copy-start.29 = (f32[256,1024]{1,0:T(8,128)S(1)}, f32[256,1024]{1,0:T(8,128)}, u32[]{:S(2)}) copy-start(f32[256,1024]{1,0:T(8,128)} %get-tuple-element.146) | copy-start | bytes 3145732
  (85 other events, 275.1 us)
Sparse Core Ops, SparseCore 0:
  25.3 33.4 all-gather.40
  61.0 24.3 all-gather.56
  87.5 23.6 all-gather.58
  122.9 34.8 reduce-scatter.30
  159.3 25.2 all-gather.60
  186.9 34.2 all-gather.42
  222.9 25.2 all-gather.62
  249.8 26.2 all-gather.64
  281.2 33.9 reduce-scatter.32
  317.7 35.1 all-gather.44
  354.5 22.2 all-gather.66
  378.2 23.4 all-gather.68
  416.0 34.7 reduce-scatter.34
  452.3 25.2 all-gather.72
  479.8 34.2 all-gather.46
  515.7 25.2 all-gather.70
  542.4 26.1 all-gather.74
  570.4 33.9 all-gather.48
  618.2 35.1 reduce-scatter.38
  656.5 35.1 all-gather.50
  782.4 35.1 reduce-scatter.40
  820.6 35.1 reduce-scatter.36
  859.8 35.1 all-gather.52
  907.5 35.1 reduce-scatter.42
  945.6 35.1 all-gather.54
  983.0 34.1 reduce-scatter.72
  1019.3 30.9 reduce-scatter.68
  1052.6 32.3 reduce-scatter.70
  1087.3 32.5 reduce-scatter.64
  1122.0 32.4 reduce-scatter.62
  1156.8 32.4 reduce-scatter.60
  1191.7 32.6 reduce-scatter.58
  1226.5 29.4 reduce-scatter.56
  1258.3 29.4 reduce-scatter.54
  1290.0 29.5 reduce-scatter.52
  1321.7 29.3 reduce-scatter.50
  1353.2 30.7 reduce-scatter.66
  1386.3 30.7 reduce-scatter.48
  1419.2 30.7 reduce-scatter.46
  1453.0 33.4 reduce-scatter.44
where the time goes:
time: 1550 us; the launch traced here: 1540 us
  waiting for transfers between devices  904 us (58%)
  matrix products  325 us (21%)
  blocking collectives  167 us (11%)
  other arithmetic  74.6 us (5%)
  local copies, waits for them, and re-layouts  49.7 us (3%)
  between operations  18.3 us (1%)
    reduce_scatter x4, waiting for transfers between devices, input_sum(): lax.psum_scatter(total_sum.astype(jnp.bfloat16), 'tp', scatter_dimension=...  135 us
    all_gather x4, waiting for transfers between devices, spread_grads(): return lax.all_gather(local_rows, 'tp', axis=0, tiled=True)  106 us
    reduce_scatter x4, waiting for transfers between devices, branch_sum(): lax.psum_scatter(mat_dot(lax.dynamic_slice_in_dim(left_arg, jnp.int32(0),...  105 us
    all_gather x4, waiting for transfers between devices, spread_rows(): return lax.all_gather(local_rows, 'tp', axis=0, tiled=True)  73.2 us
    reduce_scatter x2, waiting for transfers between devices, local(): lax.psum_scatter(grad_parts[4].astype(jnp.bfloat16), 'fsdp', scatter_dime...  67.9 us
    reduce_scatter x2, waiting for transfers between devices, local(): lax.psum_scatter(grad_parts[0].astype(jnp.bfloat16), 'fsdp', scatter_dime...  64.2 us
    reduce_scatter x2, waiting for transfers between devices, local(): lax.psum_scatter(grad_parts[1].astype(jnp.bfloat16), 'fsdp', scatter_dime...  61.6 us
    reduce_scatter x2, waiting for transfers between devices, local(): lax.psum_scatter(grad_parts[2].astype(jnp.bfloat16), 'fsdp', scatter_dime...  61.4 us
  transfers between devices with their start and end apart: 40, of which 32 were waited for; matrix products, arithmetic and copies ran while one was open for 19% of the time, Pallas kernels for 0%

commit v1 on v0

v1 whole, which is shorter than its diff:
```python
import functools
import math

import jax
import jax.numpy as jnp
from jax import lax
from jax.experimental import pallas as pl
from jax.experimental.pallas import tpu as pltpu
from jax.sharding import PartitionSpec as P

HD = 128
DOC_MAX = 512


epsilon = 1e-06
theta_base = 1000000.0


def mat_dot(left_arg, right_arg):
    return jnp.dot(left_arg, right_arg, preferred_element_type=jnp.float32)


def dot_left_t(left_arg, right_arg):
    return lax.dot_general(
        left_arg, right_arg, (((0,), (0,)), ((), ())), preferred_element_type=jnp.float32
    )


def dot_right_t(left_arg, right_arg):
    return lax.dot_general(
        left_arg, right_arg, (((1,), (1,)), ((), ())), preferred_element_type=jnp.float32
    )


def positions_of(segment_ids):
    token_index = jnp.arange(segment_ids.shape[1], dtype=jnp.int32)[None, :]
    first_flag = jnp.concatenate(
        [
            jnp.ones((segment_ids.shape[0], 1), dtype=jnp.bool_),
            segment_ids[:, 1:] != segment_ids[:, :-1],
        ],
        axis=1,
    )
    starts = lax.cummax(jnp.where(first_flag, token_index, jnp.zeros_like(token_index)), axis=1)
    return (token_index - starts).reshape(-1)


def rope_tables(positions, head_dim):
    half_dim = head_dim // 2
    frequency = jnp.exp(
        jnp.arange(half_dim, dtype=jnp.float32) * (-2.0 * math.log(theta_base) / head_dim)
    )
    angles = positions.astype(jnp.float32)[:, None] * frequency[None, :]
    return (jnp.cos(angles)[:, None, :], jnp.sin(angles)[:, None, :])


def row_norm(operand, gain_vec):
    scale_part = lax.rsqrt(jnp.mean(operand * operand, axis=-1, keepdims=True) + epsilon)
    hat_part = operand * scale_part
    return (hat_part * gain_vec, hat_part, scale_part)


def norm_back(grad_normed, hat_part, scale_part, gain_vec, sum_axes):
    scaled = grad_normed * gain_vec
    grad_in = scale_part * (scaled - hat_part * jnp.mean(scaled * hat_part, axis=-1, keepdims=True))
    grad_gain = jnp.sum(grad_normed * hat_part, axis=sum_axes)
    return (grad_in, grad_gain)


def head_rot(operand, gain_row, cos_wide, sin_wide):
    normed, hat_part, scale_part = row_norm(operand, gain_row)
    rotated = normed * cos_wide + pltpu.roll(normed, HD // 2, 1) * sin_wide
    return rotated.astype(jnp.bfloat16), hat_part, scale_part


def head_back(grad_rot, hat_part, scale_part, gain_row, cos_wide, sin_wide):
    grad_n = grad_rot * cos_wide - pltpu.roll(grad_rot, HD // 2, 1) * sin_wide
    grad_in, grad_gain = norm_back(grad_n, hat_part, scale_part, gain_row, (0,))
    return grad_in.astype(jnp.bfloat16), grad_gain[None, :]


def block_exp(q_blk, k_win, seg_col, seg_row, row_lo, key_lo):
    rows, keys = q_blk.shape[0], k_win.shape[0]
    scores = dot_right_t(q_blk, k_win) * (HD ** (-0.5))
    u_idx = row_lo + lax.broadcasted_iota(jnp.int32, (rows, keys), 0)
    t_idx = key_lo + lax.broadcasted_iota(jnp.int32, (rows, keys), 1)
    allowed = (seg_col == seg_row) & (t_idx <= u_idx)
    powers = jnp.where(allowed, jnp.exp(scores), 0.0)
    return powers / jnp.sum(powers, axis=-1, keepdims=True)


def attend_kernel(group, rows, q_ref, k_ref, v_ref, cos_ref, sin_ref, gain_ref, sc_ref, sr_ref, o_ref):
    length = k_ref.shape[0]
    gain_q, gain_k = gain_ref[0:1, :], gain_ref[1:2, :]
    k_rot, _, _ = head_rot(k_ref[...], gain_k, cos_ref[...], sin_ref[...])
    values = v_ref[...].astype(jnp.bfloat16)
    for lo in range(0, length, rows):
        hi = lo + rows
        key_lo = max(0, lo - DOC_MAX)
        for g in range(group):
            lanes = slice(g * HD, (g + 1) * HD)
            q_rot, _, _ = head_rot(
                q_ref[lo:hi, lanes], gain_q, cos_ref[lo:hi, :], sin_ref[lo:hi, :]
            )
            probs = block_exp(
                q_rot, k_rot[key_lo:hi], sc_ref[lo:hi, :], sr_ref[0, :, key_lo:hi], lo, key_lo
            )
            o_ref[lo:hi, lanes] = mat_dot(probs.astype(jnp.bfloat16), values[key_lo:hi]).astype(
                jnp.bfloat16
            )


def attend_back_kernel(
    group, rows, heads, kv, q_ref, k_ref, v_ref, cos_ref, sin_ref, gain_ref, sc_ref, sr_ref,
    da_ref, out_ref, gg_ref, dk_ref, dv_ref,
):
    length = k_ref.shape[0]
    kv_idx = pl.program_id(1)
    gain_q, gain_k = gain_ref[0:1, :], gain_ref[1:2, :]
    k_rot, k_hat, k_scale = head_rot(k_ref[...], gain_k, cos_ref[...], sin_ref[...])
    values = v_ref[...].astype(jnp.bfloat16)
    dk_ref[...] = jnp.zeros_like(dk_ref)
    dv_ref[...] = jnp.zeros_like(dv_ref)
    gq_total = jnp.zeros((1, HD), jnp.float32)
    scale = HD ** (-0.5)
    for lo in range(0, length, rows):
        hi = lo + rows
        key_lo = max(0, lo - DOC_MAX)
        k_win, v_win = k_rot[key_lo:hi], values[key_lo:hi]
        for g in range(group):
            lanes = slice(g * HD, (g + 1) * HD)
            cos_b, sin_b = cos_ref[lo:hi, :], sin_ref[lo:hi, :]
            q_rot, q_hat, q_scale = head_rot(q_ref[lo:hi, lanes], gain_q, cos_b, sin_b)
            probs = block_exp(
                q_rot, k_win, sc_ref[lo:hi, :], sr_ref[0, :, key_lo:hi], lo, key_lo
            )
            da = da_ref[lo:hi, lanes]
            dv_ref[key_lo:hi, :] += dot_left_t(probs.astype(jnp.bfloat16), da)
            grad_probs = dot_right_t(da, v_win)
            delta = jnp.sum(probs * grad_probs, axis=-1, keepdims=True)
            ds = (probs * (grad_probs - delta) * scale).astype(jnp.bfloat16)
            dk_ref[key_lo:hi, :] += dot_left_t(ds, q_rot)
            dq, gq = head_back(mat_dot(ds, k_win), q_hat, q_scale, gain_q, cos_b, sin_b)
            gq_total = gq_total + gq
            off = pl.multiple_of((kv_idx * group + g) * HD, HD)
            out_ref[lo:hi, pl.ds(off, HD)] = dq
    dk, gk = head_back(dk_ref[...], k_hat, k_scale, gain_k, cos_ref[...], sin_ref[...])
    out_ref[:, pl.ds(pl.multiple_of((heads + kv_idx) * HD, HD), HD)] = dk
    out_ref[:, pl.ds(pl.multiple_of((heads + kv + kv_idx) * HD, HD), HD)] = dv_ref[...].astype(
        jnp.bfloat16
    )

    @pl.when((pl.program_id(0) == 0) & (kv_idx == 0))
    def _():
        gg_ref[...] = jnp.zeros_like(gg_ref)

    gg_ref[0:1, :] += gq_total
    gg_ref[1:2, :] += gk


def head_specs(length, group, heads, kv):
    return [
        pl.BlockSpec((length, group * HD), lambda s, k: (s, k)),
        pl.BlockSpec((length, HD), lambda s, k: (s, heads + k)),
        pl.BlockSpec((length, HD), lambda s, k: (s, heads + kv + k)),
        pl.BlockSpec((length, HD), lambda s, k: (s, 0)),
        pl.BlockSpec((length, HD), lambda s, k: (s, 0)),
        pl.BlockSpec((8, HD), lambda s, k: (0, 0)),
        pl.BlockSpec((length, 1), lambda s, k: (s, 0)),
        pl.BlockSpec((1, 1, length), lambda s, k: (s, 0, 0)),
    ]


def attend(qkv, tables, gains, dims):
    heads, kv = dims
    cos_wide, sin_wide, seg_col, seg_row = tables
    seqs, _, length = seg_row.shape
    group = heads // kv
    rows = min(256, length)
    tokens = seqs * length
    return pl.pallas_call(
        functools.partial(attend_kernel, group, rows),
        grid=(seqs, kv),
        in_specs=head_specs(length, group, heads, kv),
        out_specs=pl.BlockSpec((length, group * HD), lambda s, k: (s, k)),
        out_shape=jax.ShapeDtypeStruct((tokens, heads * HD), jnp.bfloat16),
        cost_estimate=pl.CostEstimate(
            flops=4 * tokens * heads * HD * 640, bytes_accessed=qkv.size * 6, transcendentals=0
        ),
        compiler_params=pltpu.CompilerParams(vmem_limit_bytes=40 * 2**20),
        name="attend",
    )(qkv, qkv, qkv, cos_wide, sin_wide, gains, seg_col, seg_row)


def attend_back(qkv, tables, gains, dims, grad_attended):
    heads, kv = dims
    cos_wide, sin_wide, seg_col, seg_row = tables
    seqs, _, length = seg_row.shape
    group = heads // kv
    rows = min(256, length)
    tokens = seqs * length
    width = (heads + 2 * kv) * HD
    return pl.pallas_call(
        functools.partial(attend_back_kernel, group, rows, heads, kv),
        grid=(seqs, kv),
        in_specs=head_specs(length, group, heads, kv)
        + [pl.BlockSpec((length, group * HD), lambda s, k: (s, k))],
        out_specs=[
            pl.BlockSpec((length, width), lambda s, k: (s, 0)),
            pl.BlockSpec((8, HD), lambda s, k: (0, 0)),
        ],
        out_shape=[
            jax.ShapeDtypeStruct((tokens, width), jnp.bfloat16),
            jax.ShapeDtypeStruct((8, HD), jnp.float32),
        ],
        scratch_shapes=[pltpu.VMEM((length, HD), jnp.float32)] * 2,
        cost_estimate=pl.CostEstimate(
            flops=10 * tokens * heads * HD * 640, bytes_accessed=qkv.size * 8, transcendentals=0
        ),
        compiler_params=pltpu.CompilerParams(vmem_limit_bytes=48 * 2**20),
        name="attend_back",
    )(qkv, qkv, qkv, cos_wide, sin_wide, gains, seg_col, seg_row, grad_attended)


def spread_rows(local_rows):
    return lax.all_gather(local_rows, "tp", axis=0, tiled=True)


def sum_rows(partial_rows):
    return lax.psum_scatter(
        partial_rows.astype(jnp.bfloat16), "tp", scatter_dimension=0, tiled=True
    ).astype(jnp.float32)


def gather_weights(block):
    return lax.all_gather(block, "fsdp", axis=0, tiled=True)


def scatter_grads(block):
    return lax.psum_scatter(
        block.astype(jnp.bfloat16), "fsdp", scatter_dimension=0, tiled=True
    ).astype(jnp.float32)


def local(
    inputs, segment_ids, attn_norm, mlp_norm, query_norm, key_norm, w_query, w_key, w_value,
    w_out, w_gate, w_up, w_down, cotangent,
):
    layers = w_query.shape[0]
    fsdp = lax.axis_size("fsdp")
    fsdp_idx = lax.axis_index("fsdp")
    part = attn_norm.shape[1]
    small = query_norm.shape[1]
    q_w, kv_w = w_query.shape[2], w_key.shape[2]
    ff_w = w_gate.shape[2]
    dims = (q_w // HD, kv_w // HD)
    qkv_w = q_w + 2 * kv_w

    columns = []
    for l in range(layers):
        columns += [
            attn_norm[l],
            mlp_norm[l],
            jnp.pad(query_norm[l], (0, part - small)),
            jnp.pad(key_norm[l], (0, part - small)),
        ]
    gain_block = jnp.stack(columns, axis=1)
    gain_block = jnp.pad(gain_block, ((0, 0), (0, -gain_block.shape[1] % HD)))
    gain_w = gain_block.shape[1]

    def qkv_block(l):
        return [w_query[l], w_key[l], w_value[l]]

    def rest_block(l):
        return [w_out[l].T, w_gate[l], w_up[l], w_down[l].T]

    full = []
    for l in range(layers):
        lead = gather_weights(
            jnp.concatenate(qkv_block(l) + ([gain_block] if l == 0 else []), axis=1)
        )
        if l == 0:
            gain_all = lead[:, qkv_w:].T.astype(jnp.float32)
        rest = gather_weights(jnp.concatenate(rest_block(l), axis=1))
        full.append(
            (
                lead[:, :qkv_w],
                rest[:, :q_w],
                rest[:, q_w : q_w + ff_w],
                rest[:, q_w + ff_w : q_w + 2 * ff_w],
                rest[:, q_w + 2 * ff_w :],
            )
        )

    def gains_of(l):
        rows = gain_all[4 * l : 4 * l + 4]
        heads_gain = rows[2:].reshape(2, fsdp, part)[:, :, :small].reshape(2, fsdp * small)
        return rows[0], rows[1], jnp.pad(heads_gain, ((0, 6), (0, 0)))

    positions = positions_of(segment_ids)
    cosine, sine = rope_tables(positions, HD)
    cosine, sine = cosine[:, 0, :], sine[:, 0, :]
    seqs, length = segment_ids.shape
    tables = (
        jnp.concatenate([cosine, cosine], axis=1),
        jnp.concatenate([-sine, sine], axis=1),
        segment_ids.reshape(-1, 1),
        segment_ids.reshape(seqs, 1, length),
    )

    resid = inputs
    kept = []
    for l in range(layers):
        w_qkv, w_o, w_g, w_u, w_d = full[l]
        attn_gain, mlp_gain, head_gain = gains_of(l)
        normed, hat_a, scale_a = row_norm(resid, attn_gain)
        attn_rows = spread_rows(normed.astype(jnp.bfloat16))
        qkv = mat_dot(attn_rows, w_qkv)
        attended = attend(qkv, tables, head_gain, dims)
        resid_mid = resid + sum_rows(dot_right_t(attended, w_o))
        normed_m, hat_m, scale_m = row_norm(resid_mid, mlp_gain)
        mlp_rows = spread_rows(normed_m.astype(jnp.bfloat16))
        gate_act = mat_dot(mlp_rows, w_g)
        up_act = mat_dot(mlp_rows, w_u)
        hidden = (jax.nn.silu(gate_act) * up_act).astype(jnp.bfloat16)
        resid = resid_mid + sum_rows(dot_right_t(hidden, w_d))
        kept.append(
            (hat_a, scale_a, attn_rows, qkv, attended, hat_m, scale_m, mlp_rows, gate_act, up_act, hidden)
        )

    grad = cotangent
    grads = [None] * layers
    gain_grads = [None] * layers
    for l in reversed(range(layers)):
        w_qkv, w_o, w_g, w_u, w_d = full[l]
        attn_gain, mlp_gain, head_gain = gains_of(l)
        (hat_a, scale_a, attn_rows, qkv, attended, hat_m, scale_m, mlp_rows, gate_act, up_act, hidden) = kept[l]
        grad_half = spread_rows(grad.astype(jnp.bfloat16))
        grad_hidden = mat_dot(grad_half, w_d)
        sig = jax.nn.sigmoid(gate_act)
        grad_gate_act = (grad_hidden * up_act * sig * (1.0 + gate_act * (1.0 - sig))).astype(jnp.bfloat16)
        grad_up_act = (grad_hidden * gate_act * sig).astype(jnp.bfloat16)
        grad_normed_m = sum_rows(dot_right_t(grad_gate_act, w_g) + dot_right_t(grad_up_act, w_u))
        grad_in, grad_mlp_gain = norm_back(grad_normed_m, hat_m, scale_m, mlp_gain, (0,))
        grad_mid = grad + grad_in
        grad_mid_half = spread_rows(grad_mid.astype(jnp.bfloat16))
        grad_attended = mat_dot(grad_mid_half, w_o).astype(jnp.bfloat16)
        grad_qkv, grad_heads = attend_back(qkv, tables, head_gain, dims, grad_attended)
        grad_normed_a = sum_rows(dot_right_t(grad_qkv, w_qkv))
        grad_in, grad_attn_gain = norm_back(grad_normed_a, hat_a, scale_a, attn_gain, (0,))
        grad = grad_mid + grad_in
        rest = scatter_grads(
            jnp.concatenate(
                [
                    dot_left_t(grad_mid_half, attended).astype(jnp.bfloat16),
                    dot_left_t(mlp_rows, grad_gate_act).astype(jnp.bfloat16),
                    dot_left_t(mlp_rows, grad_up_act).astype(jnp.bfloat16),
                    dot_left_t(grad_half, hidden).astype(jnp.bfloat16),
                ],
                axis=1,
            )
        )
        lead = scatter_grads(dot_left_t(attn_rows, grad_qkv))
        grads[l] = (
            lead[:, :q_w],
            lead[:, q_w : q_w + kv_w],
            lead[:, q_w + kv_w :],
            rest[:, :q_w].T,
            rest[:, q_w : q_w + ff_w],
            rest[:, q_w + ff_w : q_w + 2 * ff_w],
            rest[:, q_w + 2 * ff_w :].T,
        )
        gain_grads[l] = jnp.concatenate(
            [grad_attn_gain, grad_mlp_gain, grad_heads[0], grad_heads[1]]
        )

    summed = lax.psum(jnp.stack(gain_grads), ("fsdp", "tp"))
    model = part * fsdp
    head = small * fsdp

    def own(lo, size, width):
        return lax.dynamic_slice_in_dim(summed[:, lo : lo + size], fsdp_idx * width, width, 1)

    stacked = [jnp.stack([grads[l][i] for l in range(layers)]) for i in range(7)]
    return (
        resid,
        grad,
        *stacked,
        own(0, model, part),
        own(model, model, part),
        own(2 * model, head, small),
        own(2 * model + head, head, small),
    )


def solution(mesh):
    return jax.shard_map(
        local,
        mesh=mesh,
        in_specs=(
            P(("fsdp", "tp"), None),
            P("fsdp", None),
            P(None, "fsdp"),
            P(None, "fsdp"),
            P(None, "fsdp"),
            P(None, "fsdp"),
            P(None, "fsdp", "tp"),
            P(None, "fsdp", "tp"),
            P(None, "fsdp", "tp"),
            P(None, "tp", "fsdp"),
            P(None, "fsdp", "tp"),
            P(None, "fsdp", "tp"),
            P(None, "tp", "fsdp"),
            P(("fsdp", "tp"), None),
        ),
        out_specs=(
            P(("fsdp", "tp"), None),
            P(("fsdp", "tp"), None),
            P(None, "fsdp", "tp"),
            P(None, "fsdp", "tp"),
            P(None, "fsdp", "tp"),
            P(None, "tp", "fsdp"),
            P(None, "fsdp", "tp"),
            P(None, "fsdp", "tp"),
            P(None, "tp", "fsdp"),
            P(None, "fsdp"),
            P(None, "fsdp"),
            P(None, "fsdp"),
            P(None, "fsdp"),
        ),
        check_vma=False,
    )
```

time: 1550 us -> 1110 us (0.72)
  matrix products: 325 us -> 116 us
  waiting for transfers between devices: 904 us -> 726 us
  blocking collectives: 167 us -> 39.8 us
  Pallas kernels: 0 us -> 67.1 us
    reduce_scatter x18 -> x10, waiting for transfers between devices: 548 us -> 303 us  [the longest x8 268 us: sum_rows(): lax.psum_scatter(partial_rows.astype(jnp.bfloat16), 'tp', scatter_dimensi...]
    all_gather x4 -> x8, waiting for transfers between devices: 73.2 us -> 235 us  [spread_rows(): return lax.all_gather(local_rows, 'tp', axis=0, tiled=True)]
    dot_general x20 -> x0, matrix products: 137 us -> none  [the longest x4 46.8 us: back_bundle(): jnp.einsum('kgqt,qkgd->tkd', grad_scores, q_rot[row_start:row_stop], pref...]
    all_gather x8 -> x0, blocking collectives: 111 us -> none  [the longest x2 33.3 us: local(): lax.all_gather(w_key[layer_idx], 'fsdp', axis=0, tiled=True)]
    all_gather x14 -> x4, waiting for transfers between devices: 248 us -> 149 us  [gather_weights(): return lax.all_gather(block, 'fsdp', axis=0, tiled=True)]
    pallas_call x0 -> x4, Pallas kernels: none -> 67.1 us  [the longest x2 43.3 us: attend_back(): pl.pallas_call(functools.partial(attend_back_kernel, group, rows, heads,...]
    unnamed x2 -> x0, blocking collectives: 40.4 us -> none
    reduce_sum x4 -> x0, matrix products: 32.5 us -> none  [attend_bundle(): totals = jnp.sum(jnp.where(allowed, jnp.exp(scores), 0.0), axis=-1)]
  transfers between devices with their start and end apart: 40 -> 24, of which waited for: 32 -> 22; matrix products, arithmetic and copies ran while one was open for 19% -> 14% of each run, Pallas kernels for 0% -> 4%
where the time goes in v1:
time: 1110 us; the launch traced here: 1100 us
  waiting for transfers between devices  726 us (65%)
  matrix products  116 us (10%)
  other arithmetic  81.2 us (7%)
  Pallas kernels  67.1 us (6%)
  local copies, waits for them, and re-layouts  55.7 us (5%)
  blocking collectives  39.8 us (4%)
  between operations  15.8 us (1%)
    reduce_scatter x8, waiting for transfers between devices, sum_rows(): lax.psum_scatter(partial_rows.astype(jnp.bfloat16), 'tp', scatter_dimensi...  268 us
    all_gather x8, waiting for transfers between devices, spread_rows(): return lax.all_gather(local_rows, 'tp', axis=0, tiled=True)  235 us
    all_gather x4, waiting for transfers between devices, gather_weights(): return lax.all_gather(block, 'fsdp', axis=0, tiled=True)  149 us
    dot_general x10, matrix products, mat_dot(): return jnp.dot(left_arg, right_arg, preferred_element_type=jnp.float32)  47.6 us
    pallas_call x2, Pallas kernels, attend_back(): pl.pallas_call(functools.partial(attend_back_kernel, group, rows, heads,...  43.3 us
    psum x1, blocking collectives, local(): summed = lax.psum(jnp.stack(gain_grads), ('fsdp', 'tp'))  39.8 us
    unnamed x26, waiting for transfers between devices  39.2 us
    dot_general x10, matrix products, dot_right_t(): lax.dot_general(left_arg, right_arg, (((1,), (1,)), ((), ())), preferred_...  38.5 us
  transfers between devices with their start and end apart: 24, of which 22 were waited for; matrix products, arithmetic and copies ran while one was open for 14% of the time, Pallas kernels for 4%

profile of v1, /device:TPU:0, one launch (start us, length us, event | category | flops | bytes accessed | tf_op | source)
XLA Modules:
  0.0 1103.9 jit_solution(15574320712082898714)
XLA Ops:
  13.9 34.1 %all-gather.13.cloned.1.call-done = bf16[1024,1152]{1,0:T(8,128)(2,1)} async-done(((bf16[128,1152]{1,0:T(8,128)(2,1)}), bf16[1024,1152]{1,0:T(8,128)(2,1)}) %all-gather.13.cloned.1.call-update) | async-done | bytes 2359312 | tf_op jit(solution)/shard_map/all_gather | solution.py:236
  58.8 27.1 %all-gather.15.cloned.1.call-done = bf16[1024,1024]{1,0:T(8,128)(2,1)} async-done(((bf16[256,1024]{1,0:T(8,128)(2,1)}), bf16[1024,1024]{1,0:T(8,128)(2,1)}) %all-gather.15.cloned.1.call-update) | async-done | bytes 2097168 | tf_op jit(solution)/shard_map/all_gather | solution.py:226
  85.9 4.5 fusion.6.q_ref.k_ref.v_ref
  90.5 11.9 %attend.2 = bf16[1024,512]{1,0:T(8,128)(2,1)S(1)} custom-call(f32[1024,1024]{1,0:T(8,128)S(1)} %fusion.6.q_ref.k_ref.v_ref, f32[1024,1024]{1,0:T(8,128)S(1)} %fusion.6.q_ref.k_ref.v_ref, f32[1024,1024]{1,0:T(8,128)S(1)} %fusion.6.q_ref.k_ref.v_ref, f32[1024,128]{1,0:T(8,128)S(1)} %get-tuple-element.137.cos_ref, f32[1024,128]{1,0:T(8,128)S(1)} %get-tuple-element.138.sin_ref, ...), custom_call_target="tpu_custom_call" | custom-call | flops 1342177280 | bytes 6291456 | tf_op jit(solution)/shard_map/attend/pallas_call | solution.py:181
  104.4 44.5 %all-gather.17.cloned.1.call-done = bf16[1024,2816]{0,1:T(8,128)(2,1)} async-done(((bf16[128,2816]{0,1:T(8,128)(2,1)}), bf16[1024,2816]{0,1:T(8,128)(2,1)}) %all-gather.17.cloned.1.call-update) | async-done | bytes 5767184 | tf_op jit(solution)/shard_map/all_gather | solution.py:236
  148.9 3.8 convolution_convert_fusion.5
  152.8 33.5 %reduce-scatter.17.cloned.1.call-done = bf16[256,1024]{1,0:T(8,128)(2,1)} async-done(((bf16[1024,1024]{1,0:T(8,128)(2,1)}), bf16[256,1024]{1,0:T(8,128)(2,1)}) %reduce-scatter.17.cloned.1.call-update) | async-done | bytes 524304 | tf_op jit(solution)/shard_map/reduce_scatter | solution.py:230
  187.6 2.0 multiply_convert_fusion.6
  189.9 35.1 %all-gather.19.cloned.1.call-done = bf16[1024,1024]{1,0:T(8,128)(2,1)} async-done(((bf16[256,1024]{1,0:T(8,128)(2,1)}), bf16[1024,1024]{1,0:T(8,128)(2,1)}) %all-gather.19.cloned.1.call-update) | async-done | bytes 2097168 | tf_op jit(solution)/shard_map/all_gather | solution.py:226
  225.0 4.0 fusion.27
  229.0 6.3 multiply_convert_fusion.3
  236.5 4.6 convolution_convert_fusion.7
  243.0 33.5 %reduce-scatter.19.cloned.1.call-done = bf16[256,1024]{1,0:T(8,128)(2,1)} async-done(((bf16[1024,1024]{1,0:T(8,128)(2,1)}), bf16[256,1024]{1,0:T(8,128)(2,1)}) %reduce-scatter.19.cloned.1.call-update) | async-done | bytes 524304 | tf_op jit(solution)/shard_map/reduce_scatter | solution.py:230
  282.1 25.7 %all-gather.23.cloned.1.call-done = bf16[1024,1024]{1,0:T(8,128)(2,1)} async-done(((bf16[128,1024]{1,0:T(8,128)(2,1)}), bf16[1024,1024]{1,0:T(8,128)(2,1)}) %all-gather.23.cloned.1.call-update) | async-done | bytes 2097168 | tf_op jit(solution)/shard_map/all_gather | solution.py:236
  307.8 37.0 %all-gather.21.cloned.1.call-done = bf16[1024,1024]{1,0:T(8,128)(2,1)} async-done(((bf16[256,1024]{1,0:T(8,128)(2,1)}), bf16[1024,1024]{1,0:T(8,128)(2,1)}) %all-gather.21.cloned.1.call-update) | async-done | bytes 2097168 | tf_op jit(solution)/shard_map/all_gather | solution.py:226
  344.8 4.5 fusion.71.q_ref.k_ref.v_ref
  349.4 11.9 %attend.3 = bf16[1024,512]{1,0:T(8,128)(2,1)S(1)} custom-call(f32[1024,1024]{1,0:T(8,128)S(1)} %fusion.71.q_ref.k_ref.v_ref, f32[1024,1024]{1,0:T(8,128)S(1)} %fusion.71.q_ref.k_ref.v_ref, f32[1024,1024]{1,0:T(8,128)S(1)} %fusion.71.q_ref.k_ref.v_ref, f32[1024,128]{1,0:T(8,128)S(1)} %get-tuple-element.137.cos_ref, ...), custom_call_target="tpu_custom_call" | custom-call | flops 1342177280 | bytes 6291456 | tf_op jit(solution)/shard_map/attend/pallas_call | solution.py:181
  363.2 44.6 %all-gather.25.cloned.1.call-done = bf16[1024,2816]{0,1:T(8,128)(2,1)} async-done(((bf16[128,2816]{0,1:T(8,128)(2,1)}), bf16[1024,2816]{0,1:T(8,128)(2,1)}) %all-gather.25.cloned.1.call-update) | async-done | bytes 5767184 | tf_op jit(solution)/shard_map/all_gather | solution.py:236
  407.8 3.8 convolution_convert_fusion.4
  411.7 2.1 convert_element_type.183
  413.9 31.3 %reduce-scatter.21.cloned.1.call-done = bf16[256,1024]{1,0:T(8,128)(2,1)} async-done(((bf16[1024,1024]{1,0:T(8,128)(2,1)}), bf16[256,1024]{1,0:T(8,128)(2,1)}) %reduce-scatter.21.cloned.1.call-update) | async-done | bytes 524304 | tf_op jit(solution)/shard_map/reduce_scatter | solution.py:230
  446.9 2.0 multiply_convert_fusion.4
  449.4 33.4 %all-gather.29.cloned.1.call-done = bf16[1024,1024]{1,0:T(8,128)(2,1)} async-done(((bf16[256,1024]{1,0:T(8,128)(2,1)}), bf16[1024,1024]{1,0:T(8,128)(2,1)}) %all-gather.29.cloned.1.call-update) | async-done | bytes 2097168 | tf_op jit(solution)/shard_map/all_gather | solution.py:226
  482.8 5.6 fusion.9
  488.4 31.9 %all-gather.27.cloned.1.call-done = bf16[1024,1024]{1,0:T(8,128)(2,1)} async-done(((bf16[256,1024]{1,0:T(8,128)(2,1)}), bf16[1024,1024]{1,0:T(8,128)(2,1)}) %all-gather.27.cloned.1.call-update) | async-done | bytes 2097168 | tf_op jit(solution)/shard_map/all_gather | solution.py:226
  520.3 4.0 fusion.13
  524.4 5.8 fusion.4
  532.0 3.2 add_convert_fusion.1
  535.3 35.3 %reduce-scatter.25.cloned.1.call-done = bf16[256,1024]{1,0:T(8,128)(2,1)} async-done(((bf16[1024,1024]{1,0:T(8,128)(2,1)}), bf16[256,1024]{1,0:T(8,128)(2,1)}) %reduce-scatter.25.cloned.1.call-update) | async-done | bytes 524304 | tf_op jit(solution)/shard_map/reduce_scatter | solution.py:230
  570.6 2.2 fusion.49
  572.8 2.4 fusion.62
  575.5 35.1 %all-gather.31.cloned.1.call-done = bf16[1024,1024]{1,0:T(8,128)(2,1)} async-done(((bf16[256,1024]{1,0:T(8,128)(2,1)}), bf16[1024,1024]{1,0:T(8,128)(2,1)}) %all-gather.31.cloned.1.call-update) | async-done | bytes 2097168 | tf_op jit(solution)/shard_map/all_gather | solution.py:226
  610.6 3.1 convolution_convert_fusion.17.da_ref
  613.7 21.5 %attend_back.2 = (bf16[1024,1024]{1,0:T(8,128)(2,1)S(1)}, f32[8,128]{1,0:T(8,128)S(1)}) custom-call(f32[1024,1024]{1,0:T(8,128)} %copy-done.1, f32[1024,1024]{1,0:T(8,128)} %copy-done.1, f32[1024,1024]{1,0:T(8,128)} %copy-done.1, f32[1024,128]{1,0:T(8,128)S(1)} %get-tuple-element.137.cos_ref, f32[1024,128]{1,0:T(8,128)S(1)} %get-tuple-element.138.sin_ref, ...), custom_call_target="tpu_custom_call" | custom-call | flops 3355443200 | bytes 8388608 | tf_op jit(solution)/shard_map/attend_back/pallas_call | solution.py:203
  636.6 3.7 convolution_convert_fusion.3
  640.6 5.0 convolution_convert_fusion.6
  645.7 30.0 %reduce-scatter.27.cloned.1.call-done = bf16[256,1024]{1,0:T(8,128)(2,1)} async-done(((bf16[1024,1024]{1,0:T(8,128)(2,1)}), bf16[256,1024]{1,0:T(8,128)(2,1)}) %reduce-scatter.27.cloned.1.call-update) | async-done | bytes 524304 | tf_op jit(solution)/shard_map/reduce_scatter | solution.py:230
  677.5 36.2 %reduce-scatter.23.cloned.1.call-done = bf16[256,1024]{1,0:T(8,128)(2,1)} async-done(((bf16[1024,1024]{1,0:T(8,128)(2,1)}), bf16[256,1024]{1,0:T(8,128)(2,1)}) %reduce-scatter.23.cloned.1.call-update) | async-done | bytes 524304 | tf_op jit(solution)/shard_map/reduce_scatter | solution.py:230
  713.7 4.3 fusion.64
  718.1 35.3 %all-gather.33.cloned.1.call-done = bf16[1024,1024]{1,0:T(8,128)(2,1)} async-done(((bf16[256,1024]{1,0:T(8,128)(2,1)}), bf16[1024,1024]{1,0:T(8,128)(2,1)}) %all-gather.33.cloned.1.call-update) | async-done | bytes 2097168 | tf_op jit(solution)/shard_map/all_gather | solution.py:226
  753.4 6.5 multiply_convert_fusion
  759.9 4.3 fusion.25
  764.3 4.6 add_convert_fusion
  768.9 35.3 %reduce-scatter.29.cloned.1.call-done = bf16[256,1024]{1,0:T(8,128)(2,1)} async-done(((bf16[1024,1024]{1,0:T(8,128)(2,1)}), bf16[256,1024]{1,0:T(8,128)(2,1)}) %reduce-scatter.29.cloned.1.call-update) | async-done | bytes 524304 | tf_op jit(solution)/shard_map/reduce_scatter | solution.py:230
  804.2 2.6 fusion.51
  806.9 2.2 fusion.63
  809.2 5.9 convolution_convert_fusion
  815.6 4.2 convolution_convert_fusion.10
  825.0 14.6 %pad_maximum_fusion.1 = bf16[1024,2816]{0,1:T(8,128)(2,1)} fusion(bf16[1024,768]{0,1:T(8,128)(2,1)S(1)} %fusion.8, bf16[1024,768]{0,1:T(8,128)(2,1)S(1)} %convolution_convert_fusion.9, bf16[1024,768]{0,1:T(8,128)(2,1)S(1)} %convolution_convert_fusion.10, bf16[1024,512]{0,1:T(8,128)(2,1)S(1)} %convolution_convert_fusion.14), kind=kLoop, calls=%fused_computation.1 | loop fusion | flops 23068672 | bytes 11534336 | tf_op jit(solution)/shard_map/concatenate | solution.py:353
  839.7 8.4 copy.68
  848.3 3.1 convolution_convert_fusion.16.da_ref
  851.5 21.7 %attend_back.3 = (bf16[1024,1024]{1,0:T(8,128)(2,1)S(1)}, f32[8,128]{1,0:T(8,128)S(1)}) custom-call(f32[1024,1024]{1,0:T(8,128)} %copy-done, f32[1024,1024]{1,0:T(8,128)} %copy-done, f32[1024,1024]{1,0:T(8,128)} %copy-done, f32[1024,128]{1,0:T(8,128)S(1)} %get-tuple-element.137.cos_ref, f32[1024,128]{1,0:T(8,128)S(1)} %get-tuple-element.138.sin_ref, ...), custom_call_target="tpu_custom_call" | custom-call | flops 3355443200 | bytes 8388608 | tf_op jit(solution)/shard_map/attend_back/pallas_call | solution.py:203
  874.5 3.7 convolution_convert_fusion.2
  878.5 6.0 convolution_convert_fusion.1
  885.9 3.6 convolution_convert_fusion.11
  894.6 14.9 %pad_maximum_fusion = bf16[1024,2816]{0,1:T(8,128)(2,1)} fusion(bf16[1024,768]{0,1:T(8,128)(2,1)S(1)} %convolution_convert_fusion.11, bf16[1024,768]{0,1:T(8,128)(2,1)S(1)} %convolution_convert_fusion.12, bf16[1024,768]{0,1:T(8,128)(2,1)S(1)} %convolution_convert_fusion.13, bf16[1024,512]{0,1:T(8,128)(2,1)S(1)} %convolution_convert_fusion.15), kind=kLoop, calls=%fused_computation | loop fusion | flops 23068672 | bytes 11534336 | tf_op jit(solution)/shard_map/concatenate | solution.py:353
  909.4 8.3 copy.66
  920.9 27.5 %reduce-scatter.39.cloned.1.call-done = bf16[128,2816]{1,0:T(8,128)(2,1)} async-done(((bf16[1024,2816]{1,0:T(8,128)(2,1)}), bf16[128,2816]{1,0:T(8,128)(2,1)}) %reduce-scatter.39.cloned.1.call-update) | async-done | bytes 720912
  952.2 32.8 %reduce-scatter.31.cloned.1.call-done = bf16[256,1024]{1,0:T(8,128)(2,1)} async-done(((bf16[1024,1024]{1,0:T(8,128)(2,1)}), bf16[256,1024]{1,0:T(8,128)(2,1)}) %reduce-scatter.31.cloned.1.call-update) | async-done | bytes 524304 | tf_op jit(solution)/shard_map/reduce_scatter | solution.py:230
  985.0 2.1 fusion.52
  988.5 34.9 %reduce-scatter.33.cloned.1.call-done = bf16[128,1024]{1,0:T(8,128)(2,1)} async-done(((bf16[1024,1024]{1,0:T(8,128)(2,1)}), bf16[128,1024]{1,0:T(8,128)(2,1)}) %reduce-scatter.33.cloned.1.call-update) | async-done | bytes 262160 | tf_op jit(solution)/shard_map/reduce_scatter | solution.py:240
  1026.5 39.8 %psum.7 = f32[2,2304]{1,0:T(2,128)} all-reduce(f32[2,2304]{1,0:T(2,128)} %pad_maximum_fusion.14), channel_id=1, replica_groups=mesh['fsdp'=8,'tp'=4] {'fsdp','tp'}, use_global_device_ids=true, to_apply=%region_26.27 | all-reduce | flops 4608 | bytes 36864 | tf_op jit(solution)/shard_map/psum | solution.py:377
  1076.3 2.3 fusion.39
  1078.6 11.4 %reduce-scatter.37.cloned.1.call-done = bf16[128,2816]{1,0:T(8,128)(2,1)} async-done(((bf16[1024,2816]{1,0:T(8,128)(2,1)}), bf16[128,2816]{1,0:T(8,128)(2,1)}) %reduce-scatter.37.cloned.1.call-update) | async-done | bytes 720912
  (296 shorter events, 81.4 us)
Async XLA Ops:
  7.2 6.5 copy-start.7
  7.2 40.8 %all-gather.13.cloned.1.call-start = ((), (), s32[]{:S(2)}) async-start(), calls=%async_computation.12 | async-start | bytes 2654208 | tf_op jit(solution)/shard_map/all_gather | solution.py:236
  13.7 72.2 %all-gather.15.cloned.1.call-start = ((), (), s32[]{:S(2)}) async-start(), calls=%async_computation.13 | async-start | bytes 2621440 | tf_op jit(solution)/shard_map/all_gather | solution.py:226
  13.9 37.4 %copy-start.46 = (f32[256]{0:T(256)}, f32[256]{0:T(256)S(1)}, u32[]{:S(2)}) copy-start(f32[256]{0:T(256)S(1)} %add_rsqrt_fusion.3) | copy-start | bytes 3076
  50.3 137.2 %copy-start.33 = (f32[1024]{0:T(1024)}, f32[1024]{0:T(1024)S(1)}, u32[]{:S(2)}) copy-start(f32[1024]{0:T(1024)S(1)} %get-tuple-element.70) | copy-start | bytes 12292
  51.3 97.6 %all-gather.17.cloned.1.call-start = ((), (), s32[]{:S(2)}) async-start(), calls=%async_computation.14 | async-start | bytes 6488064 | tf_op jit(solution)/shard_map/all_gather | solution.py:236
  54.1 132.1 %reduce-scatter.17.cloned.1.call-start = ((), (), s32[]{:S(2)}) async-start(), calls=%async_computation.15 | async-start | bytes 2621440 | tf_op jit(solution)/shard_map/reduce_scatter | solution.py:230
  104.4 48.3 %copy-start.2 = (bf16[1024,512]{1,0:T(8,128)(2,1)}, bf16[1024,512]{1,0:T(8,128)(2,1)S(1)}, u32[]{:S(2)}) copy-start(bf16[1024,512]{1,0:T(8,128)(2,1)S(1)} %attend.2) | copy-start | bytes 3145732
  152.7 33.6 %copy-start.8 = (f32[256,1024]{1,0:T(8,128)S(1)}, f32[256,1024]{1,0:T(8,128)}, u32[]{:S(2)}) copy-start(f32[256,1024]{1,0:T(8,128)} %param.14) | copy-start | bytes 3145732
  152.7 72.2 %all-gather.19.cloned.1.call-start = ((), (), s32[]{:S(2)}) async-start(), calls=%async_computation.16 | async-start | bytes 2621440 | tf_op jit(solution)/shard_map/all_gather | solution.py:226
  187.6 41.4 %copy-start.40 = (f32[256]{0:T(256)}, f32[256]{0:T(256)S(1)}, u32[]{:S(2)}) copy-start(f32[256]{0:T(256)S(1)} %add_rsqrt_fusion.2) | copy-start | bytes 3076
  189.6 86.8 %reduce-scatter.19.cloned.1.call-start = ((), (), s32[]{:S(2)}) async-start(), calls=%async_computation.17 | async-start | bytes 2621440 | tf_op jit(solution)/shard_map/reduce_scatter | solution.py:230
  225.0 4.0 copy-start.50
  229.0 6.3 copy-start.62
  241.1 35.4 %copy-start.14 = (bf16[256,1024]{1,0:T(8,128)(2,1)S(1)}, bf16[256,1024]{1,0:T(8,128)(2,1)}, u32[]{:S(2)}) copy-start(bf16[256,1024]{1,0:T(8,128)(2,1)} %reduce-scatter.17.cloned.1.call-done) | copy-start | bytes 1572868
  241.1 37.7 %copy-start.35 = (f32[1024]{0:T(1024)S(1)}, f32[1024]{0:T(1024)}, u32[]{:S(2)}) copy-start(f32[1024]{0:T(1024)} %get-tuple-element.68) | copy-start | bytes 12292
  241.1 66.7 %all-gather.23.cloned.1.call-start = ((), (), s32[]{:S(2)}) async-start(), calls=%async_computation.19 | async-start | bytes 2359296 | tf_op jit(solution)/shard_map/all_gather | solution.py:236
  242.9 101.9 %all-gather.21.cloned.1.call-start = ((), (), s32[]{:S(2)}) async-start(), calls=%async_computation.18 | async-start | bytes 2621440 | tf_op jit(solution)/shard_map/all_gather | solution.py:226
  277.8 3.2 copy-start.44
  279.7 128.1 %all-gather.25.cloned.1.call-start = ((), (), s32[]{:S(2)}) async-start(), calls=%async_computation.20 | async-start | bytes 6488064 | tf_op jit(solution)/shard_map/all_gather | solution.py:236
  281.1 164.1 %reduce-scatter.21.cloned.1.call-start = ((), (), s32[]{:S(2)}) async-start(), calls=%async_computation.21 | async-start | bytes 2621440 | tf_op jit(solution)/shard_map/reduce_scatter | solution.py:230
  411.7 35.2 %copy-start.32 = (f32[1024]{0:T(1024)S(1)}, f32[1024]{0:T(1024)}, u32[]{:S(2)}) copy-start(f32[1024]{0:T(1024)} %get-tuple-element.69) | copy-start | bytes 12292
  411.7 71.2 %all-gather.29.cloned.1.call-start = ((), (), s32[]{:S(2)}) async-start(), calls=%async_computation.24 | async-start | bytes 2621440 | tf_op jit(solution)/shard_map/all_gather | solution.py:226
  413.8 106.5 %all-gather.27.cloned.1.call-start = ((), (), s32[]{:S(2)}) async-start(), calls=%async_computation.22 | async-start | bytes 2621440 | tf_op jit(solution)/shard_map/all_gather | solution.py:226
  448.9 121.7 %reduce-scatter.25.cloned.1.call-start = ((), (), s32[]{:S(2)}) async-start(), calls=%async_computation.25 | async-start | bytes 2621440 | tf_op jit(solution)/shard_map/reduce_scatter | solution.py:230
  520.3 4.0 copy-start.53
  520.3 4.0 copy-start.58
  520.3 9.9 slice-start
  524.3 5.8 slice-start.1
  535.3 75.3 %all-gather.31.cloned.1.call-start = ((), (), s32[]{:S(2)}) async-start(), calls=%async_computation.26 | async-start | bytes 2621440 | tf_op jit(solution)/shard_map/all_gather | solution.py:226
  575.2 100.4 %reduce-scatter.27.cloned.1.call-start = ((), (), s32[]{:S(2)}) async-start(), calls=%async_computation.27 | async-start | bytes 2621440 | tf_op jit(solution)/shard_map/reduce_scatter | solution.py:230
  613.7 22.9 %copy-start.55 = (bf16[1024,1024]{1,0:T(8,128)(2,1)S(1)}, bf16[1024,1024]{1,0:T(8,128)(2,1)}, u32[]{:S(2)}) copy-start(bf16[1024,1024]{1,0:T(8,128)(2,1)} %all-gather.23.cloned.1.call-done) | copy-start | bytes 6291460
  640.3 73.4 %reduce-scatter.23.cloned.1.call-start = ((), (), s32[]{:S(2)}) async-start(), calls=%async_computation.23 | async-start | bytes 2621440 | tf_op jit(solution)/shard_map/reduce_scatter | solution.py:230
  645.6 30.0 %copy-start.36 = (f32[1024]{0:T(1024)S(1)}, f32[1024]{0:T(1024)}, u32[]{:S(2)}) copy-start(f32[1024]{0:T(1024)} %get-tuple-element.68) | copy-start | bytes 12292
  645.6 30.0 %copy-start.45 = (f32[256]{0:T(256)S(1)}, f32[256]{0:T(256)}, u32[]{:S(2)}) copy-start(f32[256]{0:T(256)} %copy-done.44) | copy-start | bytes 3076
  645.7 107.7 %all-gather.33.cloned.1.call-start = ((), (), s32[]{:S(2)}) async-start(), calls=%async_computation.28 | async-start | bytes 2621440 | tf_op jit(solution)/shard_map/all_gather | solution.py:226
  718.0 86.1 %reduce-scatter.29.cloned.1.call-start = ((), (), s32[]{:S(2)}) async-start(), calls=%async_computation.29 | async-start | bytes 2621440 | tf_op jit(solution)/shard_map/reduce_scatter | solution.py:230
  759.9 4.4 copy-start.60
  759.9 4.4 copy-start.68
  768.8 35.4 %copy-start.34 = (f32[1024]{0:T(1024)S(1)}, f32[1024]{0:T(1024)}, u32[]{:S(2)}) copy-start(f32[1024]{0:T(1024)} %copy-done.33) | copy-start | bytes 12292
  768.8 35.4 %copy-start.41 = (f32[256]{0:T(256)S(1)}, f32[256]{0:T(256)}, u32[]{:S(2)}) copy-start(f32[256]{0:T(256)} %copy-done.40) | copy-start | bytes 3076
  768.8 79.5 %all-gather.35.cloned.1.call-start = ((), (), s32[]{:S(2)}) async-start(), calls=%async_computation.30 | async-start | bytes 2621440 | tf_op jit(solution)/shard_map/all_gather | solution.py:226
  804.2 2.7 copy-start.9
  804.2 2.7 copy-start.16
  809.1 109.3 %reduce-scatter.35.cloned.1.call-start = ((), (), s32[]{:S(2)}) async-start(), calls=%async_computation.33 | async-start | bytes 2359296 | tf_op jit(solution)/shard_map/reduce_scatter | solution.py:240
  815.1 133.3 %reduce-scatter.39.cloned.1.call-start = ((), (), s32[]{:S(2)}) async-start(), calls=%async_computation.35 | async-start | bytes 6488064
  815.5 4.3 copy-start.54
  815.6 4.3 copy-start.67
  848.1 136.9 %reduce-scatter.31.cloned.1.call-start = ((), (), s32[]{:S(2)}) async-start(), calls=%async_computation.31 | async-start | bytes 2621440 | tf_op jit(solution)/shard_map/reduce_scatter | solution.py:230
  851.5 23.0 %copy-start.39 = (bf16[1024,1152]{1,0:T(8,128)(2,1)S(1)}, bf16[1024,1152]{1,0:T(8,128)(2,1)}, u32[]{:S(2)}) copy-start(bf16[1024,1152]{1,0:T(8,128)(2,1)} %all-gather.13.cloned.1.call-done) | copy-start | bytes 7077892
  878.2 145.1 %reduce-scatter.33.cloned.1.call-start = ((), (), s32[]{:S(2)}) async-start(), calls=%async_computation.32 | async-start | bytes 2359296 | tf_op jit(solution)/shard_map/reduce_scatter | solution.py:240
  884.5 205.5 %reduce-scatter.37.cloned.1.call-start = ((), (), s32[]{:S(2)}) async-start(), calls=%async_computation.34 | async-start | bytes 6488064
  885.9 3.6 copy-start.51
  885.9 3.6 copy-start.69
  949.8 35.1 %copy-start.10 = (f32[256,1024]{1,0:T(8,128)S(1)}, f32[256,1024]{1,0:T(8,128)}, u32[]{:S(2)}) copy-start(f32[256,1024]{1,0:T(8,128)} %param.14) | copy-start | bytes 3145732
  949.9 35.1 %copy-start.38 = (f32[1024]{0:T(1024)S(1)}, f32[1024]{0:T(1024)}, u32[]{:S(2)}) copy-start(f32[1024]{0:T(1024)} %copy-done.37) | copy-start | bytes 12292
  949.9 35.1 %copy-start.47 = (f32[256]{0:T(256)S(1)}, f32[256]{0:T(256)}, u32[]{:S(2)}) copy-start(f32[256]{0:T(256)} %copy-done.46) | copy-start | bytes 3076
  950.7 36.4 %copy-start.43 = (f32[1024]{0:T(1024)S(1)}, f32[1024]{0:T(1024)}, u32[]{:S(2)}) copy-start(f32[1024]{0:T(1024)} %get-tuple-element.60) | copy-start | bytes 12292
  987.0 89.2 %copy-start.17 = (f32[256,1024]{1,0:T(8,128)S(1)}, f32[256,1024]{1,0:T(8,128)}, u32[]{:S(2)}) copy-start(f32[256,1024]{1,0:T(8,128)} %get-tuple-element.73) | copy-start | bytes 3145732
  987.1 89.2 %copy-start.19 = (bf16[256,1024]{1,0:T(8,128)(2,1)S(1)}, bf16[256,1024]{1,0:T(8,128)(2,1)}, u32[]{:S(2)}) copy-start(bf16[256,1024]{1,0:T(8,128)(2,1)} %reduce-scatter.29.cloned.1.call-done) | copy-start | bytes 1572868
  987.1 89.2 %copy-start.42 = (f32[256]{0:T(256)S(1)}, f32[256]{0:T(256)}, u32[]{:S(2)}) copy-start(f32[256]{0:T(256)} %copy-done.40) | copy-start | bytes 3076
  987.9 88.4 %copy-start.49 = (f32[256]{0:T(256)S(1)}, f32[256]{0:T(256)}, u32[]{:S(2)}) copy-start(f32[256]{0:T(256)} %get-tuple-element.65) | copy-start | bytes 3076
  1066.3 9.1 copy-start.25
  1066.3 10.0 copy-start.20
  (32 other events, 56.4 us)
Sparse Core Ops, SparseCore 0:
  13.8 34.1 all-gather.12
  51.5 34.4 all-gather.14
  88.1 60.7 all-gather.16
  152.9 33.3 reduce-scatter.16
  189.8 35.1 all-gather.18
  241.2 35.1 reduce-scatter.18
  278.6 29.1 all-gather.22
  310.2 34.5 all-gather.20
  347.0 60.7 all-gather.24
  411.8 33.3 reduce-scatter.20
  447.6 35.1 all-gather.28
  485.1 35.1 all-gather.26
  535.4 35.1 reduce-scatter.24
  575.4 35.1 all-gather.30
  640.5 35.1 reduce-scatter.26
  678.5 35.1 reduce-scatter.22
  718.2 35.1 all-gather.32
  769.0 35.1 reduce-scatter.28
  809.2 35.1 all-gather.34
  846.6 36.0 reduce-scatter.34
  884.9 63.3 reduce-scatter.38
  951.3 33.6 reduce-scatter.30
  987.3 36.0 reduce-scatter.32
  1025.5 64.3 reduce-scatter.36
